TPU v7x, 256 devices: a whole 4x4x8 slice. The times are simulated.
256 devices in a mesh: rows: 32 (over y, x, core), rhs: 8 (over z).
Axes of the slice: x: 4, y: 4, z: 8, core: 2. Of those that a mesh axis runs over, the one named last changes fastest.
Arguments:
- samples: float32 [524288, 16], P(('rows', 'rhs')), may hold values from -5 to 5
- freq_table: float32 [4096, 16], replicated, may hold values from -3 to 3
- feature_seeds: int32 [512], replicated, may hold values from 0 to 4095
- phases: float32 [512], replicated, may hold values from -3.140625 to 3.140625
- treatment_features: bfloat16 [524288, 512], P('rows', 'rhs'), may hold values from -2.5 to 2.5, as said below
Outputs:
- coefficients: float32 [512, 512], replicated
- fitted: float32 [524288, 512], P(('rows', 'rhs'))
Inputs may be any that keep to these rules, and one draw needn't show every extreme that they name: `treatment_features`: treatment features depend on the instrument values.
All inputs are finite; a program needn't handle non-finite values.
Results may differ from a plain program's by a relative error of at most 0.0008.
The roundings to bfloat16 on the way count: a program that leaves them out, or rounds other values in their place, can miss the bound.
Values may be sent and summed in bfloat16 or wider, within the bound.
No kernel may reach another device: no remote copies, remote signals or barrier semaphores. Data moves between devices by JAX's collectives and lax.ppermute only.
A program may use at most 64 MiB of HBM per device.

v0:
```python
import jax
import jax.numpy as jnp
from jax import lax
from jax.sharding import Mesh
from jax.sharding import PartitionSpec as P

ROWS = ("rows_0", "rows_1", "rows_2")
ROWS_RHS = ("rows_0", "rows_1", "rows_2", "rhs")


ridge = 0.05


def rows_for(lines, length):
    spare = -lines.shape[0] % length
    if not spare:
        return lines
    return jnp.concatenate([lines, jnp.zeros((spare, *lines.shape[1:]), lines.dtype)])


def sent_to_all(array, axis):
    length = lax.axis_size(axis)
    return lax.all_to_all(
        jnp.broadcast_to(array[None], (length, *array.shape)), axis, 0, 0, tiled=True
    )


def laid_out(blocks, dim):
    blocks = jnp.moveaxis(blocks, 0, dim)
    shape = blocks.shape
    return blocks.reshape(*shape[:dim], shape[dim] * shape[dim + 1], *shape[dim + 2 :])


def whole_of(array, axes, dim):
    far, near = axes
    blocks = sent_to_all(sent_to_all(array, far), near)
    return laid_out(blocks.swapaxes(0, 1).reshape(-1, *array.shape), dim)


def split_up(array, dim, length):
    before, after = (array.shape[:dim], array.shape[dim + 1 :])
    return jnp.moveaxis(array.reshape(*before, length, -1, *after), dim, 0)


def summed_on_arrival(array, axis, dim):
    blocks = split_up(array, dim, lax.axis_size(axis))
    arrived = lax.all_to_all(blocks, axis, split_axis=0, concat_axis=0, tiled=True)
    return arrived.sum(axis=0)


def summed_rows(array, axes, dim):
    far, near = axes
    blocks = split_up(array, dim, lax.axis_size(far))
    nearer = summed_on_arrival(blocks, near, dim + 1)
    arrived = lax.all_to_all(nearer, far, split_axis=0, concat_axis=0, tiled=True)
    return arrived.sum(axis=0)


def total_of(array, axes):
    lines = array.reshape(-1, array.shape[-1])
    padded = rows_for(lines, lax.axis_size(axes[0]) * lax.axis_size(axes[1]))
    whole = whole_of(summed_rows(padded, axes, 0), axes, 0)
    return lax.slice_in_dim(whole, 0, len(lines)).reshape(array.shape)


def gather_directly(array, axis, dim):
    return laid_out(sent_to_all(array, axis), dim)


def total_of_2(array, axes):
    lines = array.reshape(-1, array.shape[-1])
    padded = rows_for(lines, lax.axis_size(axes))
    whole = gather_directly(summed_on_arrival(padded, axes, 0), axes, 0)
    return lax.slice_in_dim(whole, 0, len(lines)).reshape(array.shape)


def solve_with(factor, right):
    lower = lax.linalg.triangular_solve(factor, right, left_side=True, lower=True)
    return lax.linalg.triangular_solve(factor, lower, left_side=True, lower=True, transpose_a=True)


def features_of(values, freqs, phases):
    angles = (
        jnp.dot(
            values, freqs.T, precision=lax.Precision.HIGHEST, preferred_element_type=jnp.float32
        )
        + phases
    )
    return (jnp.sqrt(jnp.float32(2.0)) * jnp.cos(angles)).astype(jnp.bfloat16)


def body(samples, freq_table, feature_seeds, phases, treatment_features):
    own_rows = samples.shape[0]
    count = own_rows * lax.axis_size(ROWS) * lax.axis_size("rhs")
    freqs = freq_table[feature_seeds]
    contract = (((0,), (0,)), ((), ()))
    instruments = features_of(samples, freqs, phases)
    gram_part = lax.dot_general(
        instruments, instruments, contract, preferred_element_type=jnp.float32
    )
    gram = total_of(gram_part, (("rows_0", "rows_1"), ("rows_2", "rhs"))) / count
    gram = gram + ridge * jnp.eye(gram.shape[0], dtype=jnp.float32)
    factor = jnp.linalg.cholesky(gram)
    targets = lax.all_to_all(treatment_features, "rhs", split_axis=0, concat_axis=1, tiled=True)
    cross_part = lax.dot_general(instruments, targets, contract, preferred_element_type=jnp.float32)
    owned = summed_on_arrival(cross_part, "rhs", 1)
    owned = total_of_2(owned, ROWS) / count
    coefficients = gather_directly(solve_with(factor, owned), "rhs", 1)
    fitted = jnp.dot(
        instruments, coefficients.astype(jnp.bfloat16), preferred_element_type=jnp.float32
    )
    return (coefficients, fitted)


def solution(mesh):
    torus = Mesh(
        mesh.devices.reshape(4, 4, 2, mesh.shape["rhs"]), ("rows_0", "rows_1", "rows_2", "rhs")
    )
    placed = (P(ROWS_RHS, None), P(), P(), P(), P(ROWS, "rhs"))
    return jax.shard_map(
        body, mesh=torus, in_specs=placed, out_specs=(P(), P(ROWS_RHS, None)), check_vma=False
    )
```

profile of v0, /device:TPU:1, one launch (start us, length us, event | category | flops | bytes accessed | tf_op | source)
XLA Modules:
  0.0 383.9 jit_solution(17072140677375639956)
XLA Ops:
  0.7 1.6 copy.84
  2.3 1.0 gather_fusion
  3.4 17.8 %multiply_convert_fusion = bf16[512,2048]{1,0:T(8,128)(2,1)S(1)} fusion(f32[512,16]{1,0:T(8,128)S(1)} %gather_fusion, f32[2048,16]{0,1:T(8,128)S(1)} %copy-done, f32[512]{0:T(512)S(1)} %copy-done.5), kind=kOutput, calls=%fused_computation.3 | convolution fusion | flops 204472320 | bytes 2263040 | tf_op jit(solution)/shard_map/dot_general | solution.py:84
  21.2 1.3 copy-done.1
  22.5 1.3 fusion.58
  23.8 0.6 reshape_reshape.4
  24.4 0.5 copy.112
  25.0 35.8 %all_to_all.59 = f32[16,16,2,512]{3,2,1,0:T(2,128)S(1)} all-to-all(f32[16,16,2,512]{3,2,1,0:T(2,128)S(1)} %bitcast.99), channel_id=1, replica_groups=mesh['rows_0'=4,'rows_1'=4,'rows_2'=2,'rhs'=8] {'rows_2','rhs'}, dimensions={0} | all-to-all | bytes 2097152 | tf_op jit(solution)/shard_map/all_to_all | solution.py:47
  60.7 0.4 reduce_sum.36
  61.1 13.2 %all_to_all.60 = f32[16,2,512]{2,1,0:T(2,128)S(1)} all-to-all(f32[16,2,512]{2,1,0:T(2,128)S(1)} %reduce_sum.36), channel_id=1, replica_groups=mesh['rows_0'=4,'rows_1'=4,'rows_2'=2,'rhs'=8] {'rows_0','rows_1'}, dimensions={0} | all-to-all | bytes 131072 | tf_op jit(solution)/shard_map/all_to_all | solution.py:55
  74.4 0.6 broadcast_in_dim.13
  75.0 3.5 all-to-all-start.2
  78.5 1.7 copy.111
  80.3 4.7 %all-to-all-done.2 = f32[16,2,512]{2,1,0:T(2,128)S(1)} async-done(((f32[16,2,512]{2,1,0:T(2,128)}), f32[16,2,512]{2,1,0:T(2,128)S(1)}, u32[]{:S(2)}, u32[]{:S(2)}) %all-to-all-start.2) | async-done | bytes 65568 | tf_op jit(solution)/shard_map/all_to_all | solution.py:23
  85.0 51.5 %all_to_all.61 = bf16[8,2048,64]{1,2,0:T(8,128)(2,1)} all-to-all(bf16[8,2048,64]{1,2,0:T(8,128)(2,1)S(1)} %bitcast.98), channel_id=1, replica_groups=mesh['rows_0'=4,'rows_1'=4,'rows_2'=2,'rhs'=8] {'rhs'}, dimensions={0} | all-to-all | bytes 4194304 | tf_op jit(solution)/shard_map/all_to_all | solution.py:104
  136.5 1.4 broadcast_in_dim.14
  137.9 8.7 %all-to-all-start.3 = ((f32[16,16,2,512]{3,2,1,0:T(2,128)}), f32[16,16,2,512]{3,2,1,0:T(2,128)S(1)}, u32[]{:S(2)}, u32[]{:S(2)}) async-start(f32[16,16,2,512]{3,2,1,0:T(2,128)} %broadcast_in_dim.14), calls=%async_computation.3 | async-start | bytes 2097152 | tf_op jit(solution)/shard_map/all_to_all | solution.py:23
  146.6 4.5 %fusion.3 = f32[8,512,64]{1,2,0:T(8,128)} fusion(bf16[8,2048,64]{1,2,0:T(8,128)(2,1)} %all_to_all.61, bf16[512,2048]{1,0:T(8,128)(2,1)} %copy-done.1), kind=kOutput, calls=%fused_computation.8 | convolution fusion | flops 1073741824 | bytes 5242880 | tf_op jit(solution)/shard_map/dot_general | solution.py:105
  151.1 22.1 %all-to-all-done.3 = f32[16,16,2,512]{3,2,1,0:T(2,128)S(1)} async-done(((f32[16,16,2,512]{3,2,1,0:T(2,128)}), f32[16,16,2,512]{3,2,1,0:T(2,128)S(1)}, u32[]{:S(2)}, u32[]{:S(2)}) %all-to-all-start.3) | async-done | bytes 1048608 | tf_op jit(solution)/shard_map/all_to_all | solution.py:23
  173.2 4.2 %all-to-all-start.5 = ((f32[8,512,64]{1,2,0:T(8,128)}), f32[8,512,64]{1,2,0:T(8,128)S(1)}, u32[]{:S(2)}, u32[]{:S(2)}) async-start(f32[8,512,64]{1,2,0:T(8,128)} %fusion.3), calls=%async_computation.5 | async-start | bytes 2097152 | tf_op jit(solution)/shard_map/all_to_all | solution.py:47
  177.4 0.5 multiply_bitcast_fusion
  178.0 0.5 copy.87
  178.5 0.7 div.27
  179.3 0.3 copy.88
  179.6 1.1 select_add_fusion
  180.7 1.6 copy.89
  182.5 1.0 copy-done.3
  183.5 11.7 %cholesky.103 = f32[128,128]{1,0:T(8,128)S(1)} custom-call(f32[128,128]{1,0:T(8,128)S(1)} %cholesky.263), custom_call_target="Cholesky" | custom-call | tf_op jit(solution)/shard_map/jit(cholesky)/cholesky | solution.py:103
  195.2 9.8 %custom-call.32 = f32[1,128,128]{1,2,0:T(8,128)S(1)} custom-call(f32[1,128,128]{2,1,0:T(8,128)S(1)} %get-tuple-element.63), custom_call_target="InvertDiagBlocksLowerTriangular" | custom-call | tf_op jit(solution)/shard_map/jit(cholesky)/cholesky | solution.py:103
  205.1 1.2 fusion.15
  206.3 1.3 convolution_subtract_fusion
  207.8 11.9 %cholesky.215 = f32[128,128]{1,0:T(8,128)S(1)} custom-call(f32[128,128]{1,0:T(8,128)S(1)} %cholesky.267), custom_call_target="Cholesky" | custom-call | tf_op jit(solution)/shard_map/jit(cholesky)/cholesky | solution.py:103
  220.0 9.8 %custom-call.33 = f32[1,128,128]{1,2,0:T(8,128)S(1)} custom-call(f32[1,128,128]{2,1,0:T(8,128)S(1)} %get-tuple-element.61), custom_call_target="InvertDiagBlocksLowerTriangular" | custom-call | tf_op jit(solution)/shard_map/jit(cholesky)/cholesky | solution.py:103
  229.8 0.3 convolution_dynamic-update-slice_fusion
  230.2 1.5 convolution_subtract_fusion.1
  231.7 11.7 %cholesky.236 = f32[128,128]{1,0:T(8,128)S(1)} custom-call(f32[128,128]{1,0:T(8,128)S(1)} %cholesky.272), custom_call_target="Cholesky" | custom-call | tf_op jit(solution)/shard_map/jit(cholesky)/cholesky | solution.py:103
  243.5 9.8 %custom-call.34 = f32[1,128,128]{1,2,0:T(8,128)S(1)} custom-call(f32[1,128,128]{2,1,0:T(8,128)S(1)} %get-tuple-element.59), custom_call_target="InvertDiagBlocksLowerTriangular" | custom-call | tf_op jit(solution)/shard_map/jit(cholesky)/cholesky | solution.py:103
  253.7 1.3 convolution_subtract_fusion.2
  255.0 12.0 %cholesky.253 = f32[128,128]{1,0:T(8,128)S(1)} custom-call(f32[128,128]{1,0:T(8,128)S(1)} %convolution_subtract_fusion.2), custom_call_target="Cholesky" | custom-call | tf_op jit(solution)/shard_map/jit(cholesky)/cholesky | solution.py:103
  267.1 0.7 compare_reduce_fusion.2
  269.0 0.7 compare_reduce_fusion.1
  270.5 0.7 compare_reduce_fusion
  272.1 0.8 reshape.103
  273.0 4.4 %all-to-all-start.6 = ((f32[32,1,1024]{2,1,0:T(1,128)}), f32[32,1,1024]{2,1,0:T(1,128)S(1)}, u32[]{:S(2)}, u32[]{:S(2)}) async-start(f32[32,1,1024]{2,1,0:T(1,128)} %reshape.103), calls=%async_computation.6 | async-start | bytes 262144 | tf_op jit(solution)/shard_map/all_to_all | solution.py:47
  277.6 7.5 %all-to-all-done.6 = f32[32,1,1024]{2,1,0:T(1,128)S(1)} async-done(((f32[32,1,1024]{2,1,0:T(1,128)}), f32[32,1,1024]{2,1,0:T(1,128)S(1)}, u32[]{:S(2)}, u32[]{:S(2)}) %all-to-all-start.6) | async-done | bytes 131104 | tf_op jit(solution)/shard_map/all_to_all | solution.py:47
  285.0 0.6 broadcast.233
  285.6 1.0 reduce.24
  286.8 0.8 reshape.105
  287.6 3.9 %all-to-all-start.7 = ((f32[32,1,1024]{2,1,0:T(1,128)}), f32[32,1,1024]{2,1,0:T(1,128)S(1)}, u32[]{:S(2)}, u32[]{:S(2)}) async-start(f32[32,1,1024]{2,1,0:T(1,128)} %reshape.105), calls=%async_computation.7 | async-start | bytes 262144 | tf_op jit(solution)/shard_map/all_to_all | solution.py:23
  291.6 8.1 %while.1 = (s32[]{:T(128)}, f32[512,512]{0,1:T(8,128)S(1)}, s32[4,2]{0,1:T(2,128)S(1)}, f32[4,128,128]{2,1,0:T(8,128)S(1)}, s32[]{:T(128)}) while((s32[]{:T(128)}, f32[512,512]{0,1:T(8,128)S(1)}, s32[4,2]{0,1:T(2,128)S(1)}, f32[4,128,128]{2,1,0:T(8,128)S(1)}, s32[]{:T(128)}) %tuple.41), condition=%wide.while_cond, body=%wide.while_body.sunk | while | flops 2 | bytes 393321 | solution.py:79
  291.7 0.5 fusion.76
  292.2 1.3 dynamic-slice.7
  293.7 0.5 fusion.76
  294.2 1.3 dynamic-slice.7
  295.7 0.5 fusion.76
  296.3 1.3 dynamic-slice.7
  297.8 0.5 fusion.76
  298.3 1.3 dynamic-slice.7
  299.7 39.3 %custom-call.35 = f32[4,128,128]{1,2,0:T(8,128)S(1)} custom-call(f32[4,128,128]{2,1,0:T(8,128)S(1)} %get-tuple-element.9), custom_call_target="InvertDiagBlocksLowerTriangular" | custom-call | tf_op jit(solution)/shard_map/triangular_solve | solution.py:79
  339.1 1.0 reduce.25
  343.3 0.4 convolution_subtract_fusion.3
  344.1 34.8 %all_to_all.62 = f32[8,512,64]{1,2,0:T(8,128)S(1)} all-to-all(f32[8,512,64]{1,2,0:T(8,128)S(1)} %broadcast_in_dim.16), channel_id=1, replica_groups=mesh['rows_0'=4,'rows_1'=4,'rows_2'=2,'rhs'=8] {'rhs'}, dimensions={0} | all-to-all | bytes 2097152 | tf_op jit(solution)/shard_map/all_to_all | solution.py:23
  378.8 3.4 fusion.9
  382.2 1.3 copy.103
  (76 shorter events, 6.1 us)
Async XLA Ops:
  0.6 2.7 copy-start
  0.6 1.6 copy-start.4
  0.7 2.7 copy-start.5
  21.2 1.3 copy-start.1
  75.0 10.0 %all-to-all-start.2 = ((f32[16,2,512]{2,1,0:T(2,128)}), f32[16,2,512]{2,1,0:T(2,128)S(1)}, u32[]{:S(2)}, u32[]{:S(2)}) async-start(f32[16,2,512]{2,1,0:T(2,128)} %broadcast_in_dim.13), calls=%async_computation.2 | async-start | bytes 131072 | tf_op jit(solution)/shard_map/all_to_all | solution.py:23
  137.9 35.4 %all-to-all-start.3 = ((f32[16,16,2,512]{3,2,1,0:T(2,128)}), f32[16,16,2,512]{3,2,1,0:T(2,128)S(1)}, u32[]{:S(2)}, u32[]{:S(2)}) async-start(f32[16,16,2,512]{3,2,1,0:T(2,128)} %broadcast_in_dim.14), calls=%async_computation.3 | async-start | bytes 2097152 | tf_op jit(solution)/shard_map/all_to_all | solution.py:23
  173.2 98.7 %all-to-all-start.5 = ((f32[8,512,64]{1,2,0:T(8,128)}), f32[8,512,64]{1,2,0:T(8,128)S(1)}, u32[]{:S(2)}, u32[]{:S(2)}) async-start(f32[8,512,64]{1,2,0:T(8,128)} %fusion.3), calls=%async_computation.5 | async-start | bytes 2097152 | tf_op jit(solution)/shard_map/all_to_all | solution.py:47
  182.5 1.0 copy-start.3
  273.0 12.1 %all-to-all-start.6 = ((f32[32,1,1024]{2,1,0:T(1,128)}), f32[32,1,1024]{2,1,0:T(1,128)S(1)}, u32[]{:S(2)}, u32[]{:S(2)}) async-start(f32[32,1,1024]{2,1,0:T(1,128)} %reshape.103), calls=%async_computation.6 | async-start | bytes 262144 | tf_op jit(solution)/shard_map/all_to_all | solution.py:47
  287.6 51.4 %all-to-all-start.7 = ((f32[32,1,1024]{2,1,0:T(1,128)}), f32[32,1,1024]{2,1,0:T(1,128)S(1)}, u32[]{:S(2)}, u32[]{:S(2)}) async-start(f32[32,1,1024]{2,1,0:T(1,128)} %reshape.105), calls=%async_computation.7 | async-start | bytes 262144 | tf_op jit(solution)/shard_map/all_to_all | solution.py:23
  343.0 35.8 %copy-start.2 = (bf16[512,2048]{1,0:T(8,128)(2,1)S(1)}, bf16[512,2048]{1,0:T(8,128)(2,1)}, u32[]{:S(2)}) copy-start(bf16[512,2048]{1,0:T(8,128)(2,1)} %copy-done.1) | copy-start | bytes 6291460
where the time goes:
time: 391 us; the launch traced here: 384 us
  blocking collectives  135 us (35%)
  other arithmetic  123 us (31%)
  matrix products  36.3 us (9%)
  waiting for transfers between devices  34.3 us (9%)
  local copies, waits for them, and re-layouts  26 us (7%)
  starting transfers between devices  24.8 us (6%)
  between operations  4.32 us (1%)
    another operation x14, other arithmetic, body(): factor = jnp.linalg.cholesky(gram)  79 us
    all_to_all x1, blocking collectives, body(): lax.all_to_all(treatment_features, 'rhs', split_axis=0, concat_axis=1, ti...  51.5 us
    another operation x4, other arithmetic, solve_with(): lax.linalg.triangular_solve(factor, lower, left_side=True, lower=True, tr...  39.5 us
    all_to_all x1, blocking collectives, summed_on_arrival(): lax.all_to_all(blocks, axis, split_axis=0, concat_axis=0, tiled=True)  35.8 us
    all_to_all x1, blocking collectives, sent_to_all(): lax.all_to_all(jnp.broadcast_to(array[None], (length, *array.shape)), axi...  34.8 us
    all_to_all x3, waiting for transfers between devices, sent_to_all(): lax.all_to_all(jnp.broadcast_to(array[None], (length, *array.shape)), axi...  26.9 us
    dot_general x1, matrix products, features_of(): jnp.dot(values, freqs.T, precision=lax.Precision.HIGHEST, preferred_eleme...  17.8 us
    all_to_all x3, starting transfers between devices, sent_to_all(): lax.all_to_all(jnp.broadcast_to(array[None], (length, *array.shape)), axi...  16.2 us
  transfers between devices with their start and end apart: 5, of which 3 were waited for; matrix products, arithmetic and copies ran while one was open for 38% of the time, Pallas kernels for 0%

commit v1 on v0

v1 whole, which is shorter than its diff:
```python
import math

import jax
import jax.numpy as jnp
import numpy as np
from jax import lax
from jax.experimental import pallas as pl
from jax.experimental.pallas import tpu as pltpu
from jax.sharding import Mesh
from jax.sharding import PartitionSpec as P

ROWS = ("y", "x", "c")
ALL = ("y", "x", "c", "z")
RIDGE = 0.05
M = 512
TILE = 128
F32, BF16 = jnp.float32, jnp.bfloat16
MIB = 1 << 20


def sine_coefficients():
    nodes = 0.25 * np.cos(np.pi * (np.arange(400) + 0.5) / 800)
    powers = np.stack([nodes ** (2 * k + 1) for k in range(5)], 1)
    return [float(c) for c in np.linalg.lstsq(powers, np.sqrt(2) * np.sin(2 * np.pi * nodes), rcond=None)[0]]


COEFFS = sine_coefficients()


def split3(a):
    hi = a.astype(BF16)
    rest = a - hi.astype(F32)
    mid = rest.astype(BF16)
    low = (rest - mid.astype(F32)).astype(BF16)
    return hi, mid, low


def split2(a):
    hi = a.astype(BF16)
    return hi, (a - hi.astype(F32)).astype(BF16)


def dot(a, b, ca=1, cb=0):
    return lax.dot_general(a, b, (((ca,), (cb,)), ((), ())), preferred_element_type=F32)


def dot_pieces(a, b, cb=0):
    total = None
    n = len(a)
    for i in reversed(range(n)):
        for j in reversed(range(n - i)):
            term = dot(a[i], b[j], 1, cb)
            total = term if total is None else total + term
    return total


def select_frequencies(table_ref, seeds_ref, phases_ref):
    seeds = seeds_ref[...]
    near = jnp.bitwise_and(seeds, TILE - 1)
    far = jnp.right_shift(seeds, 7)
    hot = jnp.where(lax.broadcasted_iota(jnp.int32, (TILE, M), 0) == near, 1.0, 0.0).astype(BF16)
    groups = table_ref.shape[1] // TILE
    table = jnp.concatenate([table_ref[:, g * TILE : (g + 1) * TILE] for g in range(groups)], 0)
    pieces = split3(table)
    rows = (dot(pieces[0], hot) + dot(pieces[1], hot)) + dot(pieces[2], hot)
    freqs = jnp.zeros((16, M), F32)
    for g in range(groups):
        freqs = freqs + jnp.where(far == g, rows[g * 16 : (g + 1) * 16], 0.0)
    turns = F32(1 / (2 * math.pi))
    f1, f2, f3 = split3(freqs * turns)
    p1, p2, p3 = (jnp.broadcast_to(p.astype(F32), (16, M)) for p in split3(phases_ref[...] * turns))
    line = lax.broadcasted_iota(jnp.int32, (16, M), 0)
    offset = jnp.where(line == 0, p1, jnp.where(line == 1, p2, jnp.where(line == 2, p3, 0.0))).astype(BF16)
    return jnp.concatenate([f1, f2, f3, f1, f2, f1, offset], 0)


def features(x, freqs):
    x1, x2, x3 = split3(x)
    ones = jnp.ones((16, x.shape[1]), BF16)
    angle = dot(jnp.concatenate([x1, x1, x1, x2, x2, x3, ones], 0), freqs, 0, 0)
    angle = angle - jnp.round(angle)
    q = 0.25 - jnp.abs(angle)
    s = q * q
    p = COEFFS[4] * s + COEFFS[3]
    for c in COEFFS[2::-1]:
        p = p * s + c
    return (p * q).astype(BF16)


CHUNK = 256


def own_kernel(place_ref, table_ref, seeds_ref, phases_ref, x_ref, t_ref, freqs_ref, z_ref, gram_ref, cross_ref):
    freqs = select_frequencies(table_ref, seeds_ref, phases_ref)
    freqs_ref[...] = freqs
    cross = jnp.zeros(cross_ref.shape, F32)
    for k in range(0, x_ref.shape[1], CHUNK):
        z = features(x_ref[:, k : k + CHUNK], freqs)
        z_ref[k : k + CHUNK, :] = z
        cross = cross + dot(t_ref[:, k : k + CHUNK], z)
    cross_ref[...] = cross
    at = 0
    for i in range(M // TILE):
        width = (i + 1) * TILE
        block = dot(z_ref[:, i * TILE : width], z_ref[:, :width], 0, 0)
        for j in range(i + 1):
            gram_ref[at : at + TILE, :] = block[:, j * TILE : (j + 1) * TILE]
            at += TILE


def more_kernel(blocks, tiled, place_ref, freqs_ref, before_ref, *refs):
    xs, ts, out_ref = refs[:blocks], refs[blocks : 2 * blocks], refs[2 * blocks]
    freqs = freqs_ref[...]
    cross = before_ref[...]
    for x_ref, t_ref in zip(xs, ts):
        for k in range(0, x_ref.shape[1], CHUNK):
            z = features(x_ref[:, k : k + CHUNK], freqs)
            cross = cross + dot(t_ref[:, k : k + CHUNK], z)
    if tiled:
        across = M // TILE
        for r in range(out_ref.shape[0]):
            i, j = divmod(r, across)
            out_ref[r] = cross[8 * i : 8 * i + 8, TILE * j : TILE * (j + 1)]
    else:
        out_ref[...] = cross


def inverse_kernel(packed_ref, gram_ref, inverse_ref, *, scale):
    at = 0
    for i in range(M // TILE):
        for j in range(i + 1):
            block = packed_ref[at : at + TILE, :] * scale
            if i == j:
                line = lax.broadcasted_iota(jnp.int32, (TILE, TILE), 0)
                lane = lax.broadcasted_iota(jnp.int32, (TILE, TILE), 1)
                block = block + jnp.where(line == lane, F32(RIDGE), 0.0)
            gram_ref[i * TILE : (i + 1) * TILE, j * TILE : (j + 1) * TILE] = block
            if i != j:
                gram_ref[j * TILE : (j + 1) * TILE, i * TILE : (i + 1) * TILE] = block.T
            at += TILE
    gram = gram_ref[...]
    line = lax.broadcasted_iota(jnp.int32, (M, M), 0)
    lane = lax.broadcasted_iota(jnp.int32, (M, M), 1)
    twice = jnp.where(line == lane, F32(2), F32(0))
    sums = jnp.sum(jnp.abs(gram), axis=0, keepdims=True)
    top = jnp.max(sums, axis=1, keepdims=True)
    low = jnp.full((1, 1), RIDGE * 0.999, F32)
    first = 2.0 / (top + low)
    error = (top - low) / (top + low)
    gain = 2.0 / (2.0 - error * error)
    inverse_ref[...] = (gain * first) * (twice - first * gram)
    error = error * error * 0.5 * gain
    g = split2(gram)

    def more(state):
        return jnp.max(state) > 2e-3

    def step(error):
        gain = 2.0 / (2.0 - error * error)
        x = inverse_ref[...]
        pieces = split2(x)
        rest = twice - dot_pieces(g, pieces)
        inverse_ref[...] = gain * dot_pieces(pieces, split2(rest))
        return error * error * 0.5 * gain

    lax.while_loop(more, step, error)


def coefficients_kernel(gram_ref, inverse_ref, tiles_ref, out_ref, cross_ref, *, scale):
    across = M // TILE
    for r in range(tiles_ref.shape[0]):
        i, j = divmod(r, across)
        for z in range(tiles_ref.shape[1]):
            first = z * (M // tiles_ref.shape[1]) + 8 * i
            cross_ref[first : first + 8, TILE * j : TILE * (j + 1)] = tiles_ref[r, z] * scale
    cross = cross_ref[...].T
    x = split2(inverse_ref[...])
    guess = dot_pieces(x, split2(cross))
    rest = cross - dot_pieces(split3(gram_ref[...]), split3(guess))
    out_ref[...] = guess + dot_pieces(x, split2(rest))


def fitted_kernel(z_ref, coef_ref, out_ref):
    out_ref[...] = dot(z_ref[...], coef_ref[...].astype(BF16))


def params(mib=48):
    return pltpu.CompilerParams(vmem_limit_bytes=mib * MIB)


def full(shape):
    return pl.BlockSpec(shape, lambda *_: (0,) * len(shape))


def shaped(shape, dtype=F32):
    return jax.ShapeDtypeStruct(shape, dtype)


def own_part(place, table, seeds, phases, x, t):
    own, cols = x.shape[1], t.shape[0]
    return pl.pallas_call(
        own_kernel,
        grid_spec=pltpu.PrefetchScalarGridSpec(
            num_scalar_prefetch=1,
            grid=(1,),
            in_specs=[
                full(table.shape),
                full(seeds.shape),
                full(phases.shape),
                full(x.shape),
                pl.BlockSpec((cols, own), lambda _, place: (0, place[0])),
            ],
            out_specs=[full((112, M)), full((own, M)), full((1280, TILE)), full((cols, M))],
        ),
        out_shape=[shaped((112, M), BF16), shaped((own, M), BF16), shaped((1280, TILE)), shaped((cols, M))],
        compiler_params=params(),
        name="own_part",
    )(place, table, seeds, phases, x, t)


def more_cross(place, freqs, before, xs, t, tiled):
    own, cols = xs[0].shape[1], t.shape[0]
    n = len(xs)
    out = (cols * M // (8 * TILE), 8, TILE) if tiled else (cols, M)

    def kernel(*refs):
        more_kernel(n, tiled, *refs)

    return pl.pallas_call(
        kernel,
        grid_spec=pltpu.PrefetchScalarGridSpec(
            num_scalar_prefetch=1,
            grid=(1,),
            in_specs=[full(freqs.shape), full(before.shape)]
            + [full(x.shape) for x in xs]
            + [pl.BlockSpec((cols, own), lambda _, place, k=k: (0, place[k])) for k in range(n)],
            out_specs=full(out),
        ),
        out_shape=shaped(out),
        compiler_params=params(),
        name="more_cross",
    )(place, freqs, before, *xs, *([t] * n))


def whole_vmem():
    return pl.BlockSpec(memory_space=pltpu.VMEM)


def inverted(packed, count):
    def kernel(*refs):
        inverse_kernel(*refs, scale=1.0 / count)

    return pl.pallas_call(
        kernel,
        in_specs=[whole_vmem()],
        out_specs=[whole_vmem()] * 2,
        out_shape=[shaped((M, M))] * 2,
        compiler_params=params(),
        name="inverted",
    )(packed)


def solved(gram, inverse, tiles, count):
    def kernel(*refs):
        coefficients_kernel(*refs, scale=1.0 / count)

    return pl.pallas_call(
        kernel,
        in_specs=[whole_vmem()] * 3,
        out_specs=whole_vmem(),
        out_shape=shaped((M, M)),
        scratch_shapes=[pltpu.VMEM((M, M), F32)],
        compiler_params=params(),
        name="solved",
    )(gram, inverse, tiles)


def predicted(z, coef):
    own = z.shape[0]
    lines = 512
    return pl.pallas_call(
        fitted_kernel,
        grid=(own // lines,),
        in_specs=[pl.BlockSpec((lines, M), lambda i: (i, 0)), full((M, M))],
        out_specs=pl.BlockSpec((lines, M), lambda i: (i, 0)),
        out_shape=shaped((own, M)),
        compiler_params=params(),
        name="predicted",
    )(z, coef)


def to_all(array, axes):
    n = lax.axis_size(axes)
    return lax.all_to_all(jnp.broadcast_to(array[None], (n, *array.shape)), axes, 0, 0, tiled=True)


def scattered_sum(array, axes):
    return lax.all_to_all(array, axes, 0, 0, tiled=True).sum(axis=0)


def body(samples, freq_table, feature_seeds, phases, treatment_features):
    count = samples.shape[0] * lax.axis_size(ROWS) * lax.axis_size("z")
    turn = lax.axis_size("z")
    rows = lax.axis_size(ROWS)
    here = lax.axis_index("z").astype(jnp.int32)
    x = samples.T
    t = treatment_features.T

    def place(*shifts):
        return jnp.stack([lax.rem(here + (s % turn), turn) for s in shifts])

    ahead = [(k, (k + 1) % turn) for k in range(turn)]
    back = [(k, (k - 1) % turn) for k in range(turn)]
    right, left = [x], [x]
    for _ in range(turn // 2):
        right.append(lax.ppermute(right[-1], "z", ahead))
    for _ in range(turn // 2 - 1):
        left.append(lax.ppermute(left[-1], "z", back))

    freqs, z, gram_part, cross = own_part(
        place(0), freq_table.T, feature_seeds[None, :], phases[None, :], x, t
    )
    gram = scattered_sum(gram_part.reshape(rows, -1, TILE), ROWS)
    gram = to_all(gram, "z").sum(axis=0)
    gram = to_all(gram, ROWS).reshape(-1, TILE)
    for k in range(1, turn // 2 - 1):
        cross = more_cross(place(-k, k), freqs, cross, [right[k], left[k]], t, False)
    k = turn // 2 - 1
    cross = more_cross(place(-k, k, -k - 1), freqs, cross, [right[k], left[k], right[k + 1]], t, True)
    cross = scattered_sum(cross, ROWS)
    cross = to_all(to_all(cross, "z"), ROWS)
    gram, inverse = inverted(gram, count)
    coefficients = solved(gram, inverse, cross, count)
    return coefficients, predicted(z, coefficients)


def solution(mesh):
    turn = mesh.shape["rhs"]
    torus = Mesh(mesh.devices.reshape(4, 4, 2, turn), ALL)
    placed = (P(ALL, None), P(), P(), P(), P(ROWS, "z"))
    return jax.shard_map(body, mesh=torus, in_specs=placed, out_specs=(P(), P(ALL, None)), check_vma=False)
```

time: 391 us -> 163 us (0.42); the launches traced: 384 us -> 162 us
  other arithmetic: 123 us -> 1.42 us
  blocking collectives: 135 us -> 19.4 us
  Pallas kernels: 0 us -> 49.6 us
  matrix products: 36.3 us -> 0 us
  starting transfers between devices: 24.8 us -> 42.6 us
  local copies, waits for them, and re-layouts: 26 us -> 12 us
    another operation x18 -> x3, other arithmetic: 118 us -> 0.22 us  [place(): return jnp.stack([lax.rem(here + s % turn, turn) for s in shifts])]
    all_to_all x4 -> x1, blocking collectives: 135 us -> 19.4 us  [to_all(): lax.all_to_all(jnp.broadcast_to(array[None], (n, *array.shape)), axes, 0,...]
    pallas_call x0 -> x7, Pallas kernels: none -> 49.6 us  [the longest x3 25.5 us: more_cross(): pl.pallas_call(kernel, grid_spec=pltpu.PrefetchScalarGridSpec(num_scalar_...]
    dot_general x4 -> x0, matrix products: 26.9 us -> none  [the longest x1 17.8 us: features_of(): jnp.dot(values, freqs.T, precision=lax.Precision.HIGHEST, preferred_eleme...]
    ppermute x0 -> x7, starting transfers between devices: none -> 11.1 us  [the longest x3 9.38 us: body(): left.append(lax.ppermute(left[-1], 'z', back))]
    another operation x40 -> x0, local copies, waits for them, and re-layouts: 10.1 us -> none
    another operation x20 -> x0, matrix products: 9.35 us -> none  [the longest x6 5.92 us: body(): factor = jnp.linalg.cholesky(gram)]
    ppermute x0 -> x7, waiting for transfers between devices: none -> 8.81 us  [the longest x4 8.8 us: body(): right.append(lax.ppermute(right[-1], 'z', ahead))]
  transfers between devices with their start and end apart: 5 -> 12, of which waited for: 3 -> 7; matrix products, arithmetic and copies ran while one was open for 38% -> 1% of each run, Pallas kernels for 0% -> 22%
where the time goes in v1:
time: 163 us; the launch traced here: 162 us
  Pallas kernels  49.6 us (30%)
  starting transfers between devices  42.6 us (26%)
  waiting for transfers between devices  36.6 us (22%)
  blocking collectives  19.4 us (12%)
  local copies, waits for them, and re-layouts  12 us (7%)
    pallas_call x3, Pallas kernels, more_cross(): pl.pallas_call(kernel, grid_spec=pltpu.PrefetchScalarGridSpec(num_scalar_...  25.5 us
    all_to_all x3, waiting for transfers between devices, to_all(): lax.all_to_all(jnp.broadcast_to(array[None], (n, *array.shape)), axes, 0,...  21.3 us
    all_to_all x1, blocking collectives, to_all(): lax.all_to_all(jnp.broadcast_to(array[None], (n, *array.shape)), axes, 0,...  19.4 us
    all_to_all x2, starting transfers between devices, scattered_sum(): return lax.all_to_all(array, axes, 0, 0, tiled=True).sum(axis=0)  18.2 us
    all_to_all x3, starting transfers between devices, to_all(): lax.all_to_all(jnp.broadcast_to(array[None], (n, *array.shape)), axes, 0,...  13.2 us
    pallas_call x1, Pallas kernels, inverted(): pl.pallas_call(kernel, in_specs=[whole_vmem()], out_specs=[whole_vmem()]...  10.3 us
    unnamed x24, local copies, waits for them, and re-layouts  9.54 us
    ppermute x3, starting transfers between devices, body(): left.append(lax.ppermute(left[-1], 'z', back))  9.38 us
  transfers between devices with their start and end apart: 12, of which 7 were waited for; matrix products, arithmetic and copies ran while one was open for 1% of the time, Pallas kernels for 22%

profile of v1, /device:TPU:1, one launch (start us, length us, event | category | flops | bytes accessed | tf_op | source)
XLA Modules:
  0.0 162.3 jit_solution(2484348263307213233)
XLA Ops:
  0.6 0.0 copy-start
  0.6 1.6 copy-done
  2.2 0.0 copy-start.7
  2.2 0.9 copy-done.7
  3.2 0.0 copy-start.8
  3.2 0.9 copy-done.8
  4.1 0.0 copy-start.10
  4.1 0.7 copy-done.10
  4.8 0.0 copy-start.11
  4.8 0.7 copy-done.11
  5.4 0.0 copy-start.9
  5.4 0.0 copy-start.1
  5.5 5.7 %own_part.1 = (bf16[112,512]{1,0:T(8,128)(2,1)S(1)}, bf16[2048,512]{1,0:T(8,128)(2,1)S(1)}, f32[1280,128]{1,0:T(8,128)}, f32[64,512]{1,0:T(8,128)S(1)}) custom-call(s32[1]{0:T(128)} %bitcast.place_ref, f32[16,4096]{1,0:T(8,128)S(1)} %bitcast.24, s32[1,512]{1,0:T(1,128)S(1)} %bitcast.28, f32[1,512]{1,0:T(1,128)S(1)} %bitcast.29, f32[16,2048]{1,0:T(8,128)S(1)} %bitcast.25, ...), custom_call_target="tpu_custom_call" | custom-call | tf_op jit(solution)/shard_map/own_part/pallas_call | solution.py:201
  11.1 0.0 copy-start.3
  11.1 1.3 copy-done.3
  12.4 8.6 %all-to-all-start = ((f32[32,40,128]{2,1,0:T(8,128)}), f32[32,40,128]{2,1,0:T(8,128)}, u32[]{:S(2)}, u32[]{:S(2)}) async-start(f32[32,40,128]{2,1,0:T(8,128)} %bitcast.6), calls=%async_computation | async-start | bytes 1310720 | tf_op jit(solution)/shard_map/all_to_all | solution.py:298
  21.1 0.0 copy-done.9
  21.1 1.7 %collective-permute-start = (f32[16,2048]{1,0:T(8,128)S(1)}, f32[16,2048]{1,0:T(8,128)S(1)}, u32[]{:S(2)}, u32[]{:S(2)}) collective-permute-start(f32[16,2048]{1,0:T(8,128)S(1)} %bitcast.26), channel_id=1, source_target_pairs={{0,1},{1,2},{2,3},{3,4},{4,5},{5,6},{6,7},{7,0},{8,9},{9,10},{10,1... | collective-permute-start | bytes 393224 | tf_op jit(solution)/shard_map/ppermute | solution.py:316
  22.8 4.0 %collective-permute-start.1 = (f32[16,2048]{1,0:T(8,128)S(1)}, f32[16,2048]{1,0:T(8,128)S(1)}, u32[]{:S(2)}, u32[]{:S(2)}) collective-permute-start(f32[16,2048]{1,0:T(8,128)S(1)} %bitcast.27), channel_id=1, source_target_pairs={{0,7},{1,0},{2,1},{3,2},{4,3},{5,4},{6,5},{7,6},{8,15},{9,8},{10,9... | collective-permute-start | bytes 393224 | tf_op jit(solution)/shard_map/ppermute | solution.py:318
  26.9 3.7 %collective-permute-done.refs_3_ = f32[16,2048]{1,0:T(8,128)S(1)} collective-permute-done((f32[16,2048]{1,0:T(8,128)S(1)}, f32[16,2048]{1,0:T(8,128)S(1)}, u32[]{:S(2)}, u32[]{:S(2)}) %collective-permute-start) | collective-permute-done | bytes 131104 | tf_op jit(solution)/shard_map/ppermute | solution.py:316
  30.5 0.0 collective-permute-start.2
  30.5 0.0 collective-permute-done.1.refs_4_
  30.5 2.7 %collective-permute-start.3 = (f32[16,2048]{1,0:T(8,128)S(1)}, f32[16,2048]{1,0:T(8,128)S(1)}, u32[]{:S(2)}, u32[]{:S(2)}) collective-permute-start(f32[16,2048]{1,0:T(8,128)S(1)} %collective-permute-done.1.refs_4_), channel_id=1, source_target_pairs={{0,7},{1,0},{2,1},{3,2},{4,3},{5,4},{6,5},{7,6},{8,15},{9,8},{10,9... | collective-permute-start | bytes 393224 | tf_op jit(solution)/shard_map/ppermute | solution.py:318
  33.2 2.9 %collective-permute-done.2.refs_3_ = f32[16,2048]{1,0:T(8,128)S(1)} collective-permute-done((f32[16,2048]{1,0:T(8,128)S(1)}, f32[16,2048]{1,0:T(8,128)S(1)}, u32[]{:S(2)}, u32[]{:S(2)}) %collective-permute-start.2) | collective-permute-done | bytes 131104 | tf_op jit(solution)/shard_map/ppermute | solution.py:316
  36.1 0.0 collective-permute-start.4
  36.1 0.1 pad_add_fusion.1.refs_0_
  36.1 0.0 collective-permute-done.3.refs_4_
  36.1 2.7 %collective-permute-start.5 = (f32[16,2048]{1,0:T(8,128)S(1)}, f32[16,2048]{1,0:T(8,128)S(1)}, u32[]{:S(2)}, u32[]{:S(2)}) collective-permute-start(f32[16,2048]{1,0:T(8,128)S(1)} %collective-permute-done.3.refs_4_), channel_id=1, source_target_pairs={{0,7},{1,0},{2,1},{3,2},{4,3},{5,4},{6,5},{7,6},{8,15},{9,8},{10,9... | collective-permute-start | bytes 393224 | tf_op jit(solution)/shard_map/ppermute | solution.py:318
  38.8 2.3 %collective-permute-done.4.refs_3_ = f32[16,2048]{1,0:T(8,128)S(1)} collective-permute-done((f32[16,2048]{1,0:T(8,128)S(1)}, f32[16,2048]{1,0:T(8,128)S(1)}, u32[]{:S(2)}, u32[]{:S(2)}) %collective-permute-start.4) | collective-permute-done | bytes 131104 | tf_op jit(solution)/shard_map/ppermute | solution.py:316
  41.1 0.0 collective-permute-start.6
  41.1 0.1 pad_add_fusion.2.refs_0_
  41.2 0.1 pad_add_fusion.refs_0_
  41.3 0.0 copy-done.1
  41.3 7.1 %more_cross.3.refs_2_ = f32[64,512]{1,0:T(8,128)S(1)} custom-call(s32[2]{0:T(128)S(1)} %pad_add_fusion.2.refs_0_, bf16[112,512]{1,0:T(8,128)(2,1)S(1)} %get-tuple-element.11.refs_1_, f32[64,512]{1,0:T(8,128)S(1)} %get-tuple-element.12.refs_2_, f32[16,2048]{1,0:T(8,128)S(1)} %collective-permute-done.refs_3_, f32[16,2048]{1,0:T(8,128)S(1)} %collective-permute-done.1.refs_4_, ...), custom_call_target="tpu_custom_call" | custom-call | tf_op jit(solution)/shard_map/more_cross/pallas_call | solution.py:229
  48.4 7.1 %more_cross.4.refs_2_ = f32[64,512]{1,0:T(8,128)S(1)} custom-call(s32[2]{0:T(128)S(1)} %pad_add_fusion.1.refs_0_, bf16[112,512]{1,0:T(8,128)(2,1)S(1)} %get-tuple-element.11.refs_1_, f32[64,512]{1,0:T(8,128)S(1)} %more_cross.3.refs_2_, f32[16,2048]{1,0:T(8,128)S(1)} %collective-permute-done.2.refs_3_, f32[16,2048]{1,0:T(8,128)S(1)} %collective-permute-done.3.refs_4_, ...), custom_call_target="tpu_custom_call" | custom-call | tf_op jit(solution)/shard_map/more_cross/pallas_call | solution.py:229
  55.6 0.0 collective-permute-done.5.refs_4_
  55.6 0.0 collective-permute-done.6.refs_5_
  55.6 11.2 %more_cross.5 = f32[32,8,128]{2,1,0:T(8,128)} custom-call(s32[3]{0:T(128)S(1)} %pad_add_fusion.refs_0_, bf16[112,512]{1,0:T(8,128)(2,1)S(1)} %get-tuple-element.11.refs_1_, f32[64,512]{1,0:T(8,128)S(1)} %more_cross.4.refs_2_, f32[16,2048]{1,0:T(8,128)S(1)} %collective-permute-done.4.refs_3_, f32[16,2048]{1,0:T(8,128)S(1)} %collective-permute-done.5.refs_4_, ...), custom_call_target="tpu_custom_call" | custom-call | tf_op jit(solution)/shard_map/more_cross/pallas_call | solution.py:229
  66.8 0.0 all-to-all-done
  66.8 9.6 %all-to-all-start.3 = ((f32[32,8,128]{2,1,0:T(8,128)}), f32[32,8,128]{2,1,0:T(8,128)S(1)}, u32[]{:S(2)}, u32[]{:S(2)}) async-start(f32[32,8,128]{2,1,0:T(8,128)} %more_cross.5), calls=%async_computation.3 | async-start | bytes 262144 | tf_op jit(solution)/shard_map/all_to_all | solution.py:298
  76.4 1.1 reduce_sum.27
  77.5 6.5 %all-to-all-done.3 = f32[32,8,128]{2,1,0:T(8,128)S(1)} async-done(((f32[32,8,128]{2,1,0:T(8,128)}), f32[32,8,128]{2,1,0:T(8,128)S(1)}, u32[]{:S(2)}, u32[]{:S(2)}) %all-to-all-start.3) | async-done | bytes 131104 | tf_op jit(solution)/shard_map/all_to_all | solution.py:298
  84.0 0.7 broadcast_in_dim.14
  84.7 5.8 %all-to-all-start.1 = ((f32[8,40,128]{2,1,0:T(8,128)}), f32[8,40,128]{2,1,0:T(8,128)S(1)}, u32[]{:S(2)}, u32[]{:S(2)}) async-start(f32[8,40,128]{2,1,0:T(8,128)} %broadcast_in_dim.14), calls=%async_computation.1 | async-start | bytes 327680 | tf_op jit(solution)/shard_map/all_to_all | solution.py:294
  90.5 8.5 %all-to-all-done.1 = f32[8,40,128]{2,1,0:T(8,128)S(1)} async-done(((f32[8,40,128]{2,1,0:T(8,128)}), f32[8,40,128]{2,1,0:T(8,128)S(1)}, u32[]{:S(2)}, u32[]{:S(2)}) %all-to-all-start.1) | async-done | bytes 163872 | tf_op jit(solution)/shard_map/all_to_all | solution.py:294
  99.0 0.6 broadcast_in_dim.16
  99.6 3.3 %all-to-all-start.4 = ((f32[8,8,128]{2,1,0:T(8,128)}), f32[8,8,128]{2,1,0:T(8,128)S(1)}, u32[]{:S(2)}, u32[]{:S(2)}) async-start(f32[8,8,128]{2,1,0:T(8,128)} %broadcast_in_dim.16), calls=%async_computation.4 | async-start | bytes 65536 | tf_op jit(solution)/shard_map/all_to_all | solution.py:294
  103.0 6.8 %all-to-all-done.4 = f32[8,8,128]{2,1,0:T(8,128)S(1)} async-done(((f32[8,8,128]{2,1,0:T(8,128)}), f32[8,8,128]{2,1,0:T(8,128)S(1)}, u32[]{:S(2)}, u32[]{:S(2)}) %all-to-all-start.4) | async-done | bytes 32800 | tf_op jit(solution)/shard_map/all_to_all | solution.py:294
  109.8 19.4 %all_to_all.30 = f32[32,40,128]{2,1,0:T(8,128)S(1)} all-to-all(f32[32,40,128]{2,1,0:T(8,128)S(1)} %broadcast_in_dim.15), channel_id=1, replica_groups=mesh['y'=4,'x'=4,'c'=2,'z'=8] {'y','x','c'}, dimensions={0} | all-to-all | bytes 1310720 | tf_op jit(solution)/shard_map/all_to_all | solution.py:294
  129.2 1.1 broadcast_in_dim.17
  130.3 4.1 %all-to-all-start.5 = ((f32[32,8,8,128]{3,2,1,0:T(8,128)}), f32[32,8,8,128]{3,2,1,0:T(8,128)S(1)}, u32[]{:S(2)}, u32[]{:S(2)}) async-start(f32[32,8,8,128]{3,2,1,0:T(8,128)} %broadcast_in_dim.17), calls=%async_computation.5 | async-start | bytes 2097152 | tf_op jit(solution)/shard_map/all_to_all | solution.py:294
  134.4 10.3 %inverted.1 = (f32[512,512]{1,0:T(8,128)S(1)}, f32[512,512]{1,0:T(8,128)S(1)}) custom-call(f32[1280,128]{1,0:T(8,128)S(1)} %bitcast.23), custom_call_target="tpu_custom_call" | custom-call | tf_op jit(solution)/shard_map/inverted/pallas_call | solution.py:253
  144.7 0.0 copy-start.5
  144.7 1.0 copy-done.5
  145.7 6.0 %all-to-all-done.5.refs_2_ = f32[32,8,8,128]{3,2,1,0:T(8,128)S(1)} async-done(((f32[32,8,8,128]{3,2,1,0:T(8,128)}), f32[32,8,8,128]{3,2,1,0:T(8,128)S(1)}, u32[]{:S(2)}, u32[]{:S(2)}) %all-to-all-start.5) | async-done | bytes 1048608 | tf_op jit(solution)/shard_map/all_to_all | solution.py:294
  151.7 0.0 copy-start.6
  151.7 1.2 copy-done.6
  152.9 0.0 copy-start.4
  152.9 4.8 %solved.1.coef_ref = f32[512,512]{1,0:T(8,128)} custom-call(f32[512,512]{1,0:T(8,128)S(1)} %get-tuple-element.9.refs_0_, f32[512,512]{1,0:T(8,128)S(1)} %copy-done.6, f32[32,8,8,128]{3,2,1,0:T(8,128)S(1)} %all-to-all-done.5.refs_2_), custom_call_target="tpu_custom_call" | custom-call | tf_op jit(solution)/shard_map/solved/pallas_call | solution.py:267
  157.8 0.0 copy-done.4
  157.8 0.0 copy-start.2
  157.8 1.2 copy-done.2
  159.0 3.3 %predicted.1 = f32[2048,512]{1,0:T(8,128)} custom-call(bf16[2048,512]{1,0:T(8,128)(2,1)S(1)} %copy-done.4, f32[512,512]{1,0:T(8,128)S(1)} %copy-done.2), custom_call_target="tpu_custom_call" | custom-call | tf_op jit(solution)/shard_map/predicted/pallas_call | solution.py:281
  (3 shorter events, 0.1 us)
Async XLA Ops:
  0.6 1.6 copy-start
  2.2 0.9 copy-start.7
  3.2 0.9 copy-start.8
  4.1 0.7 copy-start.10
  4.8 0.7 copy-start.11
  5.4 15.6 %copy-start.9 = (f32[2048,16]{0,1:T(8,128)S(1)}, f32[2048,16]{0,1:T(8,128)}, u32[]{:S(2)}) copy-start(f32[2048,16]{0,1:T(8,128)} %param.5) | copy-start | bytes 393220
  5.4 35.8 %copy-start.1 = (bf16[16384,64]{0,1:T(8,128)(2,1)S(1)}, bf16[16384,64]{0,1:T(8,128)(2,1)}, u32[]{:S(2)}) copy-start(bf16[16384,64]{0,1:T(8,128)(2,1)} %param.9) | copy-start | bytes 6291460
  11.1 1.3 copy-start.3
  12.4 54.4 %all-to-all-start = ((f32[32,40,128]{2,1,0:T(8,128)}), f32[32,40,128]{2,1,0:T(8,128)}, u32[]{:S(2)}, u32[]{:S(2)}) async-start(f32[32,40,128]{2,1,0:T(8,128)} %bitcast.6), calls=%async_computation | async-start | bytes 1310720 | tf_op jit(solution)/shard_map/all_to_all | solution.py:298
  21.1 9.4 %collective-permute-start = (f32[16,2048]{1,0:T(8,128)S(1)}, f32[16,2048]{1,0:T(8,128)S(1)}, u32[]{:S(2)}, u32[]{:S(2)}) collective-permute-start(f32[16,2048]{1,0:T(8,128)S(1)} %bitcast.26), channel_id=1, source_target_pairs={{0,1},{1,2},{2,3},{3,4},{4,5},{5,6},{6,7},{7,0},{8,9},{9,10},{10,1... | collective-permute-start | bytes 393224 | tf_op jit(solution)/shard_map/ppermute | solution.py:316
  22.8 7.7 %collective-permute-start.1 = (f32[16,2048]{1,0:T(8,128)S(1)}, f32[16,2048]{1,0:T(8,128)S(1)}, u32[]{:S(2)}, u32[]{:S(2)}) collective-permute-start(f32[16,2048]{1,0:T(8,128)S(1)} %bitcast.27), channel_id=1, source_target_pairs={{0,7},{1,0},{2,1},{3,2},{4,3},{5,4},{6,5},{7,6},{8,15},{9,8},{10,9... | collective-permute-start | bytes 393224 | tf_op jit(solution)/shard_map/ppermute | solution.py:318
  30.5 5.5 %collective-permute-start.2 = (f32[16,2048]{1,0:T(8,128)S(1)}, f32[16,2048]{1,0:T(8,128)S(1)}, u32[]{:S(2)}, u32[]{:S(2)}) collective-permute-start(f32[16,2048]{1,0:T(8,128)S(1)} %collective-permute-done.refs_3_), channel_id=1, source_target_pairs={{0,1},{1,2},{2,3},{3,4},{4,5},{5,6},{6,7},{7,0},{8,9},{9,10},{10,1... | collective-permute-start | bytes 393224 | tf_op jit(solution)/shard_map/ppermute | solution.py:316
  30.5 5.6 %collective-permute-start.3 = (f32[16,2048]{1,0:T(8,128)S(1)}, f32[16,2048]{1,0:T(8,128)S(1)}, u32[]{:S(2)}, u32[]{:S(2)}) collective-permute-start(f32[16,2048]{1,0:T(8,128)S(1)} %collective-permute-done.1.refs_4_), channel_id=1, source_target_pairs={{0,7},{1,0},{2,1},{3,2},{4,3},{5,4},{6,5},{7,6},{8,15},{9,8},{10,9... | collective-permute-start | bytes 393224 | tf_op jit(solution)/shard_map/ppermute | solution.py:318
  36.1 5.0 %collective-permute-start.4 = (f32[16,2048]{1,0:T(8,128)S(1)}, f32[16,2048]{1,0:T(8,128)S(1)}, u32[]{:S(2)}, u32[]{:S(2)}) collective-permute-start(f32[16,2048]{1,0:T(8,128)S(1)} %collective-permute-done.2.refs_3_), channel_id=1, source_target_pairs={{0,1},{1,2},{2,3},{3,4},{4,5},{5,6},{6,7},{7,0},{8,9},{9,10},{10,1... | collective-permute-start | bytes 393224 | tf_op jit(solution)/shard_map/ppermute | solution.py:316
  36.1 19.4 %collective-permute-start.5 = (f32[16,2048]{1,0:T(8,128)S(1)}, f32[16,2048]{1,0:T(8,128)S(1)}, u32[]{:S(2)}, u32[]{:S(2)}) collective-permute-start(f32[16,2048]{1,0:T(8,128)S(1)} %collective-permute-done.3.refs_4_), channel_id=1, source_target_pairs={{0,7},{1,0},{2,1},{3,2},{4,3},{5,4},{6,5},{7,6},{8,15},{9,8},{10,9... | collective-permute-start | bytes 393224 | tf_op jit(solution)/shard_map/ppermute | solution.py:318
  41.1 14.5 %collective-permute-start.6 = (f32[16,2048]{1,0:T(8,128)S(1)}, f32[16,2048]{1,0:T(8,128)S(1)}, u32[]{:S(2)}, u32[]{:S(2)}) collective-permute-start(f32[16,2048]{1,0:T(8,128)S(1)} %collective-permute-done.4.refs_3_), channel_id=1, source_target_pairs={{0,1},{1,2},{2,3},{3,4},{4,5},{5,6},{6,7},{7,0},{8,9},{9,10},{10,1... | collective-permute-start | bytes 393224 | tf_op jit(solution)/shard_map/ppermute | solution.py:316
  66.8 17.2 %all-to-all-start.3 = ((f32[32,8,128]{2,1,0:T(8,128)}), f32[32,8,128]{2,1,0:T(8,128)S(1)}, u32[]{:S(2)}, u32[]{:S(2)}) async-start(f32[32,8,128]{2,1,0:T(8,128)} %more_cross.5), calls=%async_computation.3 | async-start | bytes 262144 | tf_op jit(solution)/shard_map/all_to_all | solution.py:298
  84.7 14.3 %all-to-all-start.1 = ((f32[8,40,128]{2,1,0:T(8,128)}), f32[8,40,128]{2,1,0:T(8,128)S(1)}, u32[]{:S(2)}, u32[]{:S(2)}) async-start(f32[8,40,128]{2,1,0:T(8,128)} %broadcast_in_dim.14), calls=%async_computation.1 | async-start | bytes 327680 | tf_op jit(solution)/shard_map/all_to_all | solution.py:294
  99.6 10.1 %all-to-all-start.4 = ((f32[8,8,128]{2,1,0:T(8,128)}), f32[8,8,128]{2,1,0:T(8,128)S(1)}, u32[]{:S(2)}, u32[]{:S(2)}) async-start(f32[8,8,128]{2,1,0:T(8,128)} %broadcast_in_dim.16), calls=%async_computation.4 | async-start | bytes 65536 | tf_op jit(solution)/shard_map/all_to_all | solution.py:294
  130.3 21.4 %all-to-all-start.5 = ((f32[32,8,8,128]{3,2,1,0:T(8,128)}), f32[32,8,8,128]{3,2,1,0:T(8,128)S(1)}, u32[]{:S(2)}, u32[]{:S(2)}) async-start(f32[32,8,8,128]{3,2,1,0:T(8,128)} %broadcast_in_dim.17), calls=%async_computation.5 | async-start | bytes 2097152 | tf_op jit(solution)/shard_map/all_to_all | solution.py:294
  144.7 1.0 copy-start.5
  151.7 1.2 copy-start.6
  152.9 4.8 %copy-start.4 = (bf16[2048,512]{1,0:T(8,128)(2,1)S(1)}, bf16[2048,512]{1,0:T(8,128)(2,1)}, u32[]{:S(2)}) copy-start(bf16[2048,512]{1,0:T(8,128)(2,1)} %copy-done.3) | copy-start | bytes 6291460
  157.8 1.2 copy-start.2

commit v2 on v1

v2 whole, which is shorter than its diff:
```python
import math

import jax
import jax.numpy as jnp
import numpy as np
from jax import lax
from jax.experimental import pallas as pl
from jax.experimental.pallas import tpu as pltpu
from jax.sharding import Mesh
from jax.sharding import PartitionSpec as P

ROWS = ("y", "x", "c")
ALL = ("y", "x", "c", "z")
RIDGE = 0.05
M = 512
TILE = 128
F32, BF16 = jnp.float32, jnp.bfloat16
MIB = 1 << 20


def sine_coefficients():
    nodes = 0.25 * np.cos(np.pi * (np.arange(400) + 0.5) / 800)
    powers = np.stack([nodes ** (2 * k + 1) for k in range(5)], 1)
    return [float(c) for c in np.linalg.lstsq(powers, np.sqrt(2) * np.sin(2 * np.pi * nodes), rcond=None)[0]]


COEFFS = sine_coefficients()


def split3(a):
    hi = a.astype(BF16)
    rest = a - hi.astype(F32)
    mid = rest.astype(BF16)
    low = (rest - mid.astype(F32)).astype(BF16)
    return hi, mid, low


def split2(a):
    hi = a.astype(BF16)
    return hi, (a - hi.astype(F32)).astype(BF16)


def dot(a, b, ca=1, cb=0):
    return lax.dot_general(a, b, (((ca,), (cb,)), ((), ())), preferred_element_type=F32)


def dot_pieces(a, b, cb=0):
    total = None
    n = len(a)
    for i in reversed(range(n)):
        for j in reversed(range(n - i)):
            term = dot(a[i], b[j], 1, cb)
            total = term if total is None else total + term
    return total


def select_frequencies(table_ref, seeds_ref, phases_ref):
    seeds = seeds_ref[...]
    near = jnp.bitwise_and(seeds, TILE - 1)
    far = jnp.right_shift(seeds, 7)
    hot = jnp.where(lax.broadcasted_iota(jnp.int32, (TILE, M), 0) == near, 1.0, 0.0).astype(BF16)
    groups = table_ref.shape[1] // TILE
    table = jnp.concatenate([table_ref[:, g * TILE : (g + 1) * TILE] for g in range(groups)], 0)
    pieces = split3(table)
    rows = (dot(pieces[0], hot) + dot(pieces[1], hot)) + dot(pieces[2], hot)
    freqs = jnp.zeros((16, M), F32)
    for g in range(groups):
        freqs = freqs + jnp.where(far == g, rows[g * 16 : (g + 1) * 16], 0.0)
    turns = F32(1 / (2 * math.pi))
    f1, f2, f3 = split3(freqs * turns)
    p1, p2, p3 = (jnp.broadcast_to(p.astype(F32), (16, M)) for p in split3(phases_ref[...] * turns))
    line = lax.broadcasted_iota(jnp.int32, (16, M), 0)
    offset = jnp.where(line == 0, p1, jnp.where(line == 1, p2, jnp.where(line == 2, p3, 0.0))).astype(BF16)
    return jnp.concatenate([f1, f2, f3, f1, f2, f1, offset], 0)


def stacked(x):
    x1, x2, x3 = split3(x)
    return jnp.concatenate([x1, x1, x1, x2, x2, x3, jnp.ones((16, x.shape[1]), BF16)], 0)


def cosines(angle):
    angle = angle - jnp.round(angle)
    q = 0.25 - jnp.abs(angle)
    s = q * q
    p = COEFFS[4] * s + COEFFS[3]
    for c in COEFFS[2::-1]:
        p = p * s + c
    return (p * q).astype(BF16)


CHUNK = 512


def copied(pairs, sems):
    copies = [pltpu.make_async_copy(src, dst, sems.at[k]) for k, (src, dst) in enumerate(pairs)]
    for copy in copies:
        copy.start()
    return copies


def add_block(x, freqs, panel, lhs, z):
    for c in range(0, z.shape[0], CHUNK):
        span = slice(c, c + CHUNK)
        pieces = stacked(x[:, span])
        z[span, :] = cosines(dot(pieces, freqs, 0, 0))
        lhs[lhs.shape[0] - panel.shape[0] :, span] = cosines(dot(panel, pieces))


def block_of(t_hbm, shift, turn, own):
    at = pl.multiple_of(lax.rem(lax.axis_index("z") + shift % turn, turn) * own, own)
    return t_hbm.at[:, pl.ds(at, own)]


def own_kernel(turn, table_hbm, seeds_hbm, phases_hbm, x_hbm, t_hbm, *refs):
    freqs_ref, panel_ref, total_ref, z_hbm, table, seeds, phases, x, z, lhs, sems = refs
    own, cols = z.shape[0], t_hbm.shape[0]
    pairs = [(table_hbm, table), (seeds_hbm, seeds), (phases_hbm, phases), (x_hbm, x)]
    pairs.append((block_of(t_hbm, 0, turn, own), lhs.at[:cols]))
    copies = copied(pairs, sems)
    for copy in copies[:4]:
        copy.wait()
    freqs = select_frequencies(table, seeds, phases)
    freqs_ref[...] = freqs
    wide = panel_ref.shape[0]
    line = lax.broadcasted_iota(jnp.int32, (wide, M), 0) + wide * lax.axis_index("z")
    chosen = jnp.where(line == lax.broadcasted_iota(jnp.int32, (wide, M), 1), 1.0, 0.0).astype(BF16)
    panel = dot(chosen, freqs, 1, 1).astype(BF16)
    panel_ref[...] = panel
    add_block(x, freqs, panel, lhs, z)
    out = pltpu.make_async_copy(z, z_hbm, sems.at[5])
    out.start()
    copies[4].wait()
    total_ref[...] = dot(lhs[...], z[...])
    out.wait()


def more_kernel(shifts, tiled, turn, freqs_ref, panel_ref, before_ref, t_hbm, *refs):
    n = len(shifts)
    xs, (out_ref, lhs, z, sems) = refs[:n], refs[n:]
    own, cols = z.shape[0], t_hbm.shape[0]
    copies = copied([(block_of(t_hbm, s, turn, own), lhs.at[k, :cols]) for k, s in enumerate(shifts)], sems)
    freqs, panel = freqs_ref[...], panel_ref[...]
    total = before_ref[...]
    for k, x_ref in enumerate(xs):
        add_block(x_ref, freqs, panel, lhs.at[k], z)
        copies[k].wait()
        total = total + dot(lhs[k], z[...])
    if tiled:
        across = M // TILE
        for r in range(out_ref.shape[0]):
            i, j = divmod(r, across)
            lanes = slice(TILE * j, TILE * (j + 1))
            out_ref[r, :8] = total[cols + 8 * i : cols + 8 * i + 8, lanes]
            out_ref[r, 8:] = total[8 * i : 8 * i + 8, lanes]
    else:
        out_ref[...] = total


PANELS = 6


def panel_of(block, k):
    return 2 * ((block + k // 2) % (M // TILE)) + k % 2


def pack_kernel(parts_ref, gram_ref, cross_ref):
    column = (2 * lax.axis_index("x") + lax.axis_index("c")) % (M // TILE)
    for k in range(PANELS):
        tile = parts_ref[panel_of(column, k)][:8]
        for r in range(gram_ref.shape[0]):
            gram_ref[r, k] = tile
    for z in range(parts_ref.shape[0]):
        tile = parts_ref[z, 8:]
        for r in range(cross_ref.shape[0]):
            cross_ref[r, z] = tile


def spread_kernel(parts, out_ref):
    total = parts[0]
    for k in range(1, parts.shape[0]):
        total = total + parts[k]
    for k in range(out_ref.shape[0]):
        out_ref[k] = total


def inverse_kernel(scale, packed_ref, inverse_ref, gram_ref):
    across = M // TILE
    for r in range(packed_ref.shape[0]):
        i, j = divmod(r, across)
        for k in range(PANELS):
            first = 64 * panel_of(j, k) + 8 * i
            gram_ref[first : first + 8, TILE * j : TILE * (j + 1)] = packed_ref[r, k] * scale
    for i in range(across):
        j = (i + 1) % across
        lower = slice(TILE * i, TILE * (i + 1)), slice(TILE * j, TILE * (j + 1))
        gram_ref[lower] = gram_ref[lower[::-1]].T
    line = lax.broadcasted_iota(jnp.int32, (M, M), 0)
    lane = lax.broadcasted_iota(jnp.int32, (M, M), 1)
    twice = jnp.where(line == lane, F32(2), F32(0))
    gram = gram_ref[...] + (RIDGE / 2) * twice
    gram_ref[...] = gram
    sums = jnp.sum(jnp.abs(gram), axis=0, keepdims=True)
    top = jnp.max(sums, axis=1, keepdims=True)
    low = jnp.full((1, 1), RIDGE * 0.999, F32)
    first = 2.0 / (top + low)
    error = (top - low) / (top + low)
    gain = 2.0 / (2.0 - error * error)
    inverse_ref[...] = (gain * first) * (twice - first * gram)
    error = error * error * 0.5 * gain
    g = split2(gram)

    def more(state):
        return jnp.max(state) > 2e-3

    def step(error):
        gain = 2.0 / (2.0 - error * error)
        x = inverse_ref[...]
        pieces = split2(x)
        rest = twice - dot_pieces(g, pieces)
        inverse_ref[...] = gain * dot_pieces(pieces, split2(rest))
        return error * error * 0.5 * gain

    lax.while_loop(more, step, error)
    x = inverse_ref[...]
    rest = twice - dot_pieces(split3(gram_ref[...]), split3(x))
    inverse_ref[...] = dot_pieces(split2(x), split2(rest))


def finish_kernel(scale, inverse_ref, tiles, z_hbm, coef_ref, fitted_hbm, cross_ref, z, fitted, sems):
    n = z.shape[0]
    lines = z.shape[1]
    spans = [pl.ds(k * lines, lines) for k in range(n)]
    copies = copied([(z_hbm.at[span], z.at[k]) for k, span in enumerate(spans)], sems)
    x = split2(inverse_ref[...])
    across = M // TILE
    for r in range(tiles.shape[0]):
        i, j = divmod(r, across)
        for k in range(tiles.shape[1]):
            first = k * (M // tiles.shape[1]) + 8 * i
            cross_ref[first : first + 8, TILE * j : TILE * (j + 1)] = tiles[r, k] * scale
    coef = dot_pieces(x, split2(cross_ref[...]), 1)
    coef_ref[...] = coef
    low = coef.astype(BF16)
    outs = []
    for k, span in enumerate(spans):
        copies[k].wait()
        fitted[k] = dot(z[k], low)
        out = pltpu.make_async_copy(fitted.at[k], fitted_hbm.at[span], sems.at[n + k])
        out.start()
        outs.append(out)
    for out in outs:
        out.wait()


def cost(us):
    return pl.CostEstimate(flops=int(us * 1.15e9), transcendentals=0, bytes_accessed=0)


def params(mib=48):
    return pltpu.CompilerParams(vmem_limit_bytes=mib * MIB)


def full(shape):
    return pl.BlockSpec(shape, lambda *_: (0,) * len(shape))


def shaped(shape, dtype=F32):
    return jax.ShapeDtypeStruct(shape, dtype)


HBM = pl.BlockSpec(memory_space=pltpu.HBM)
VMEM = pl.BlockSpec(memory_space=pltpu.VMEM)


def in_hbm(array):
    return pltpu.with_memory_space_constraint(array, pltpu.HBM)


def own_part(table, seeds, phases, x, t, turn):
    own, cols = x.shape[1], t.shape[0]
    wide = M // turn
    ins = (table, seeds, phases, x)

    def kernel(*refs):
        own_kernel(turn, *refs)

    return pl.pallas_call(
        kernel,
        in_specs=[HBM] * 5,
        out_specs=[VMEM, VMEM, VMEM, HBM],
        out_shape=[shaped((112, M), BF16), shaped((wide, 112), BF16), shaped((cols + wide, M)), shaped((own, M), BF16)],
        scratch_shapes=[pltpu.VMEM(a.shape, a.dtype) for a in ins]
        + [pltpu.VMEM((own, M), BF16), pltpu.VMEM((cols + wide, own), BF16), pltpu.SemaphoreType.DMA((6,))],
        compiler_params=params(),
        cost_estimate=cost(5),
        name="own_part",
    )(*(in_hbm(a) for a in ins), in_hbm(t))


def more_part(shifts, freqs, panel, before, xs, t, turn, tiled=False):
    own, cols = xs[0].shape[1], t.shape[0]
    n = len(xs)
    lines = before.shape[0]
    out = (cols * M // (8 * TILE), 8 * lines // cols, TILE) if tiled else before.shape

    def kernel(*refs):
        more_kernel(shifts, tiled, turn, *refs)

    return pl.pallas_call(
        kernel,
        in_specs=[VMEM, VMEM, VMEM, HBM] + [VMEM] * n,
        out_specs=VMEM,
        out_shape=shaped(out),
        scratch_shapes=[
            pltpu.VMEM((n, lines, own), BF16),
            pltpu.VMEM((own, M), BF16),
            pltpu.SemaphoreType.DMA((n,)),
        ],
        compiler_params=params(),
        cost_estimate=cost(2.6 * n),
        name="more_part",
    )(freqs, panel, before, in_hbm(t), *xs)


def spread(parts, copies):
    return pl.pallas_call(
        spread_kernel,
        in_specs=[VMEM],
        out_specs=VMEM,
        out_shape=shaped((copies, *parts.shape[1:])),
        compiler_params=params(),
        cost_estimate=cost(1),
        name="spread",
    )(parts)


def packed(parts, rows):
    return pl.pallas_call(
        pack_kernel,
        in_specs=[VMEM],
        out_specs=[VMEM, VMEM],
        out_shape=[shaped((rows, PANELS, 8, TILE)), shaped((rows, parts.shape[0], 8, TILE))],
        compiler_params=params(),
        cost_estimate=cost(1),
        name="packed",
    )(parts)


def inverted(tiles, count):
    def kernel(*refs):
        inverse_kernel(1.0 / count, *refs)

    return pl.pallas_call(
        kernel,
        in_specs=[VMEM],
        out_specs=VMEM,
        out_shape=shaped((M, M)),
        scratch_shapes=[pltpu.VMEM((M, M), F32)],
        compiler_params=params(),
        cost_estimate=cost(16),
        name="inverted",
    )(tiles)


def finished(inverse, tiles, z, count):
    own = z.shape[0]
    n = 4
    lines = own // n

    def kernel(*refs):
        finish_kernel(1.0 / count, *refs)

    return pl.pallas_call(
        kernel,
        in_specs=[VMEM, VMEM, HBM],
        out_specs=[VMEM, HBM],
        out_shape=[shaped((M, M)), shaped((own, M))],
        scratch_shapes=[
            pltpu.VMEM((M, M), F32),
            pltpu.VMEM((n, lines, M), BF16),
            pltpu.VMEM((n, lines, M), F32),
            pltpu.SemaphoreType.DMA((2 * n,)),
        ],
        compiler_params=params(),
        cost_estimate=cost(4),
        name="finished",
    )(inverse, tiles, z)


def exchanged(array, axes):
    return lax.all_to_all(array, axes, 0, 0, tiled=True)


def body(samples, freq_table, feature_seeds, phases, treatment_features):
    count = samples.shape[0] * lax.axis_size(ROWS) * lax.axis_size("z")
    turn = lax.axis_size("z")
    rows = lax.axis_size(ROWS)
    x = samples.T
    t = treatment_features.T

    ahead = [(k, (k + 1) % turn) for k in range(turn)]
    back = [(k, (k - 1) % turn) for k in range(turn)]
    right, left = [x], [x]
    half = turn // 2
    for _ in range(half):
        right.append(lax.ppermute(right[-1], "z", ahead))
    for _ in range(half - 1):
        left.append(lax.ppermute(left[-1], "z", back))

    freqs, panel, total, z = own_part(freq_table.T, feature_seeds[None, :], phases[None, :], x, t, turn)
    for k in range(1, half):
        total = more_part((-k, k), freqs, panel, total, (right[k], left[k]), t, turn)
    total = more_part((-half,), freqs, panel, total, (right[half],), t, turn, tiled=True)
    parts = exchanged(spread(exchanged(total, ROWS), turn), "z")
    gram, cross = packed(parts, rows)
    inverse = inverted(exchanged(gram, ROWS), count)
    cross = exchanged(cross, ROWS)
    return finished(inverse, cross, z, count)


def solution(mesh):
    turn = mesh.shape["rhs"]
    torus = Mesh(mesh.devices.reshape(4, 4, 2, turn), ALL)
    placed = (P(ALL, None), P(), P(), P(), P(ROWS, "z"))
    return jax.shard_map(body, mesh=torus, in_specs=placed, out_specs=(P(), P(ALL, None)), check_vma=False)
```

time: 163 us -> 118 us (0.72)
  waiting for transfers between devices: 36.6 us -> 4.22 us
  blocking collectives: 19.4 us -> 49.8 us
  starting transfers between devices: 42.6 us -> 16.6 us
  local copies, waits for them, and re-layouts: 12 us -> 2.9 us
  Pallas kernels: 49.6 us -> 43.5 us
    all_to_all x1 -> x3, blocking collectives: 19.4 us -> 49.8 us  [exchanged(): return lax.all_to_all(array, axes, 0, 0, tiled=True)]
    all_to_all x5 -> x1, starting transfers between devices: 31.4 us -> 4.15 us  [exchanged(): return lax.all_to_all(array, axes, 0, 0, tiled=True)]
    all_to_all x5 -> x1, waiting for transfers between devices: 27.8 us -> 4.21 us  [exchanged(): return lax.all_to_all(array, axes, 0, 0, tiled=True)]
    ppermute x4, waiting for transfers between devices: 8.8 us -> 0.01 us  [body(): right.append(lax.ppermute(right[-1], 'z', ahead))]
    unnamed x24 -> x4, local copies, waits for them, and re-layouts: 9.54 us -> 2.9 us
    pallas_call x7 -> x9, Pallas kernels: 49.6 us -> 43.5 us  [the longest x4 19.7 us: more_part(): pl.pallas_call(kernel, in_specs=[VMEM, VMEM, VMEM, HBM] + [VMEM] * n, out...]
    ppermute x3, starting transfers between devices: 9.38 us -> 12.1 us  [body(): left.append(lax.ppermute(left[-1], 'z', back))]
    broadcast_in_dim x4 -> x0, local copies, waits for them, and re-layouts: 2.46 us -> none  [to_all(): jnp.broadcast_to(array[None], (n, *array.shape))]
  transfers between devices with their start and end apart: 12 -> 8, of which waited for: 7 -> 1; matrix products, arithmetic and copies ran while one was open for 1% -> 0% of each run, Pallas kernels for 22% -> 29%
where the time goes in v2:
time: 118 us
  blocking collectives  49.8 us (42%)
  Pallas kernels  43.5 us (37%)
  starting transfers between devices  16.6 us (14%)
  waiting for transfers between devices  4.22 us (4%)
  local copies, waits for them, and re-layouts  2.9 us (2%)
    all_to_all x3, blocking collectives, exchanged(): return lax.all_to_all(array, axes, 0, 0, tiled=True)  49.8 us
    pallas_call x4, Pallas kernels, more_part(): pl.pallas_call(kernel, in_specs=[VMEM, VMEM, VMEM, HBM] + [VMEM] * n, out...  19.7 us
    pallas_call x1, Pallas kernels, inverted(): pl.pallas_call(kernel, in_specs=[VMEM], out_specs=VMEM, out_shape=shaped(...  13.1 us
    ppermute x3, starting transfers between devices, body(): left.append(lax.ppermute(left[-1], 'z', back))  12.1 us
    pallas_call x1, Pallas kernels, finished(): pl.pallas_call(kernel, in_specs=[VMEM, VMEM, HBM], out_specs=[VMEM, HBM],...  4.92 us
    pallas_call x1, Pallas kernels, own_part(): pl.pallas_call(kernel, in_specs=[HBM] * 5, out_specs=[VMEM, VMEM, VMEM, H...  4.73 us
    all_to_all x1, waiting for transfers between devices, exchanged(): return lax.all_to_all(array, axes, 0, 0, tiled=True)  4.21 us
    all_to_all x1, starting transfers between devices, exchanged(): return lax.all_to_all(array, axes, 0, 0, tiled=True)  4.15 us
  transfers between devices with their start and end apart: 8, of which 1 were waited for; matrix products, arithmetic and copies ran while one was open for 0% of the time, Pallas kernels for 29%

profile of v2, /device:TPU:1, one launch (start us, length us, event | category | flops | bytes accessed | tf_op | source)
XLA Modules:
  0.0 117.9 jit_solution(7883764827350946699)
XLA Ops:
  0.6 6.5 %collective-permute-start.1 = (f32[16,2048]{1,0:T(8,128)}, f32[16,2048]{1,0:T(8,128)S(1)}, u32[]{:S(2)}, u32[]{:S(2)}) collective-permute-start(f32[16,2048]{1,0:T(8,128)} %bitcast.11), channel_id=1, source_target_pairs={{0,7},{1,0},{2,1},{3,2},{4,3},{5,4},{6,5},{7,6},{8,15},{9,8},{10,9... | collective-permute-start | bytes 393224 | tf_op jit(solution)/shard_map/ppermute | solution.py:409
  7.1 0.0 collective-permute-start
  7.1 4.7 %own_part.1 = (bf16[112,512]{1,0:T(8,128)(2,1)S(1)}, bf16[64,112]{1,0:T(8,128)(2,1)S(1)}, f32[128,512]{1,0:T(8,128)S(1)}, bf16[2048,512]{1,0:T(8,128)(2,1)S(1)}) custom-call(f32[16,4096]{1,0:T(8,128)} %bitcast.10, s32[1,512]{1,0:T(1,128)} %bitcast.14, f32[1,512]{1,0:T(1,128)} %bitcast.15, f32[16,2048]{1,0:T(8,128)} %bitcast.13, bf16[64,16384]{1,0:T(8,128)(2,1)} %bitcast.5), custom_call_target="tpu_custom_call" | custom-call | flops 5750000128 | tf_op jit(solution)/shard_map/own_part/pallas_call | solution.py:288
  11.9 0.0 copy-start
  11.9 1.3 %copy-done = bf16[2048,512]{1,0:T(8,128)(2,1)} copy-done((bf16[2048,512]{1,0:T(8,128)(2,1)}, bf16[2048,512]{1,0:T(8,128)(2,1)S(1)}, u32[]{:S(2)}) %copy-start) | copy-done | bytes 2097176
  13.2 0.0 collective-permute-done.1.refs_5_
  13.2 2.7 %collective-permute-start.3 = (f32[16,2048]{1,0:T(8,128)S(1)}, f32[16,2048]{1,0:T(8,128)S(1)}, u32[]{:S(2)}, u32[]{:S(2)}) collective-permute-start(f32[16,2048]{1,0:T(8,128)S(1)} %collective-permute-done.1.refs_5_), channel_id=1, source_target_pairs={{0,7},{1,0},{2,1},{3,2},{4,3},{5,4},{6,5},{7,6},{8,15},{9,8},{10,9... | collective-permute-start | bytes 393224 | tf_op jit(solution)/shard_map/ppermute | solution.py:409
  15.9 0.0 collective-permute-done.refs_4_
  15.9 0.0 collective-permute-start.2
  15.9 5.6 %more_part.4.refs_2_ = f32[128,512]{1,0:T(8,128)S(1)} custom-call(bf16[112,512]{1,0:T(8,128)(2,1)S(1)} %get-tuple-element.8.refs_0_, bf16[64,112]{1,0:T(8,128)(2,1)S(1)} %get-tuple-element.9.refs_1_, f32[128,512]{1,0:T(8,128)S(1)} %get-tuple-element.10.refs_2_, bf16[64,16384]{1,0:T(8,128)(2,1)} %bitcast.6, f32[16,2048]{1,0:T(8,128)S(1)} %collective-permute-done.refs_4_, ...), custom_call_target="tpu_custom_call" | custom-call | flops 5980000256 | tf_op jit(solution)/shard_map/more_part/pallas_call | solution.py:310
  21.5 0.0 collective-permute-done.3.refs_5_
  21.5 2.9 %collective-permute-start.5 = (f32[16,2048]{1,0:T(8,128)S(1)}, f32[16,2048]{1,0:T(8,128)S(1)}, u32[]{:S(2)}, u32[]{:S(2)}) collective-permute-start(f32[16,2048]{1,0:T(8,128)S(1)} %collective-permute-done.3.refs_5_), channel_id=1, source_target_pairs={{0,7},{1,0},{2,1},{3,2},{4,3},{5,4},{6,5},{7,6},{8,15},{9,8},{10,9... | collective-permute-start | bytes 393224 | tf_op jit(solution)/shard_map/ppermute | solution.py:409
  24.4 0.0 collective-permute-done.2.refs_4_
  24.4 0.0 collective-permute-start.4
  24.4 5.6 %more_part.5.refs_2_ = f32[128,512]{1,0:T(8,128)S(1)} custom-call(bf16[112,512]{1,0:T(8,128)(2,1)S(1)} %get-tuple-element.8.refs_0_, bf16[64,112]{1,0:T(8,128)(2,1)S(1)} %get-tuple-element.9.refs_1_, f32[128,512]{1,0:T(8,128)S(1)} %more_part.4.refs_2_, bf16[64,16384]{1,0:T(8,128)(2,1)} %bitcast.7, f32[16,2048]{1,0:T(8,128)S(1)} %collective-permute-done.2.refs_4_, ...), custom_call_target="tpu_custom_call" | custom-call | flops 5980000256 | tf_op jit(solution)/shard_map/more_part/pallas_call | solution.py:310
  30.0 0.0 collective-permute-done.4.refs_4_
  30.0 0.3 collective-permute-start.6
  30.3 0.0 collective-permute-done.5.refs_5_
  30.3 5.6 %more_part.6.refs_2_ = f32[128,512]{1,0:T(8,128)S(1)} custom-call(bf16[112,512]{1,0:T(8,128)(2,1)S(1)} %get-tuple-element.8.refs_0_, bf16[64,112]{1,0:T(8,128)(2,1)S(1)} %get-tuple-element.9.refs_1_, f32[128,512]{1,0:T(8,128)S(1)} %more_part.5.refs_2_, bf16[64,16384]{1,0:T(8,128)(2,1)} %bitcast.8, f32[16,2048]{1,0:T(8,128)S(1)} %collective-permute-done.4.refs_4_, ...), custom_call_target="tpu_custom_call" | custom-call | flops 5980000256 | tf_op jit(solution)/shard_map/more_part/pallas_call | solution.py:310
  35.9 0.0 collective-permute-done.6.refs_4_
  35.9 2.9 %more_part.7 = f32[32,16,128]{2,1,0:T(8,128)S(1)} custom-call(bf16[112,512]{1,0:T(8,128)(2,1)S(1)} %get-tuple-element.8.refs_0_, bf16[64,112]{1,0:T(8,128)(2,1)S(1)} %get-tuple-element.9.refs_1_, f32[128,512]{1,0:T(8,128)S(1)} %more_part.6.refs_2_, bf16[64,16384]{1,0:T(8,128)(2,1)} %bitcast.9, f32[16,2048]{1,0:T(8,128)S(1)} %collective-permute-done.6.refs_4_), custom_call_target="tpu_custom_call" | custom-call | flops 2990000128 | tf_op jit(solution)/shard_map/more_part/pallas_call | solution.py:310
  38.8 18.7 %all_to_all.20.parts = f32[32,16,128]{2,1,0:T(8,128)S(1)} all-to-all(f32[32,16,128]{2,1,0:T(8,128)S(1)} %more_part.7), channel_id=1, replica_groups=mesh['y'=4,'x'=4,'c'=2,'z'=8] {'y','x','c'}, dimensions={0} | all-to-all | bytes 524288 | tf_op jit(solution)/shard_map/all_to_all | solution.py:392
  57.6 11.9 %all_to_all.21.parts_ref = f32[8,16,128]{2,1,0:T(8,128)S(1)} all-to-all(f32[8,16,128]{2,1,0:T(8,128)S(1)} %spread.1), channel_id=1, replica_groups=mesh['y'=4,'x'=4,'c'=2,'z'=8] {'z'}, dimensions={0} | all-to-all | bytes 131072 | tf_op jit(solution)/shard_map/all_to_all | solution.py:392
  69.4 1.1 packed.1
  70.5 19.2 %all_to_all.22.refs_0_ = f32[32,6,8,128]{3,2,1,0:T(8,128)S(1)} all-to-all(f32[32,6,8,128]{3,2,1,0:T(8,128)S(1)} %get-tuple-element.11), channel_id=1, replica_groups=mesh['y'=4,'x'=4,'c'=2,'z'=8] {'y','x','c'}, dimensions={0} | all-to-all | bytes 1572864 | tf_op jit(solution)/shard_map/all_to_all | solution.py:392
  89.7 4.2 %all-to-all-start.3 = ((f32[32,8,8,128]{3,2,1,0:T(8,128)}), f32[32,8,8,128]{3,2,1,0:T(8,128)S(1)}, u32[]{:S(2)}, u32[]{:S(2)}) async-start(f32[32,8,8,128]{3,2,1,0:T(8,128)} %get-tuple-element.12), calls=%async_computation.3 | async-start | bytes 2097152 | tf_op jit(solution)/shard_map/all_to_all | solution.py:392
  93.9 13.1 %inverted.1.refs_0_ = f32[512,512]{1,0:T(8,128)S(1)} custom-call(f32[32,6,8,128]{3,2,1,0:T(8,128)S(1)} %all_to_all.22.refs_0_), custom_call_target="tpu_custom_call" | custom-call | flops 18400000000 | tf_op jit(solution)/shard_map/inverted/pallas_call | solution.py:354
  107.0 4.2 %all-to-all-done.3.refs_1_ = f32[32,8,8,128]{3,2,1,0:T(8,128)S(1)} async-done(((f32[32,8,8,128]{3,2,1,0:T(8,128)}), f32[32,8,8,128]{3,2,1,0:T(8,128)S(1)}, u32[]{:S(2)}, u32[]{:S(2)}) %all-to-all-start.3) | async-done | bytes 1048608 | tf_op jit(solution)/shard_map/all_to_all | solution.py:392
  111.2 0.0 copy-start.1
  111.2 1.6 %copy-done.1 = bf16[2048,512]{1,0:T(8,128)(2,1)S(1)} copy-done((bf16[2048,512]{1,0:T(8,128)(2,1)S(1)}, bf16[2048,512]{1,0:T(8,128)(2,1)}, u32[]{:S(2)}) %copy-start.1) | copy-done | bytes 2097176
  112.8 4.9 %finished.1 = (f32[512,512]{1,0:T(8,128)}, f32[2048,512]{1,0:T(8,128)}) custom-call(f32[512,512]{1,0:T(8,128)S(1)} %inverted.1.refs_0_, f32[32,8,8,128]{3,2,1,0:T(8,128)S(1)} %all-to-all-done.3.refs_1_, bf16[2048,512]{1,0:T(8,128)(2,1)S(1)} %copy-done.1), custom_call_target="tpu_custom_call" | custom-call | flops 4600000000 | tf_op jit(solution)/shard_map/finished/pallas_call | solution.py:374
  (1 shorter events, 0.0 us)
Async XLA Ops:
  0.6 12.5 %collective-permute-start.1 = (f32[16,2048]{1,0:T(8,128)}, f32[16,2048]{1,0:T(8,128)S(1)}, u32[]{:S(2)}, u32[]{:S(2)}) collective-permute-start(f32[16,2048]{1,0:T(8,128)} %bitcast.11), channel_id=1, source_target_pairs={{0,7},{1,0},{2,1},{3,2},{4,3},{5,4},{6,5},{7,6},{8,15},{9,8},{10,9... | collective-permute-start | bytes 393224 | tf_op jit(solution)/shard_map/ppermute | solution.py:409
  7.1 8.7 %collective-permute-start = (f32[16,2048]{1,0:T(8,128)}, f32[16,2048]{1,0:T(8,128)S(1)}, u32[]{:S(2)}, u32[]{:S(2)}) collective-permute-start(f32[16,2048]{1,0:T(8,128)} %bitcast.12), channel_id=1, source_target_pairs={{0,1},{1,2},{2,3},{3,4},{4,5},{5,6},{6,7},{7,0},{8,9},{9,10},{10,1... | collective-permute-start | bytes 393224 | tf_op jit(solution)/shard_map/ppermute | solution.py:407
  11.9 1.3 %copy-start = (bf16[2048,512]{1,0:T(8,128)(2,1)}, bf16[2048,512]{1,0:T(8,128)(2,1)S(1)}, u32[]{:S(2)}) copy-start(bf16[2048,512]{1,0:T(8,128)(2,1)S(1)} %get-tuple-element.13.refs_2_) | copy-start | bytes 6291460
  13.2 8.3 %collective-permute-start.3 = (f32[16,2048]{1,0:T(8,128)S(1)}, f32[16,2048]{1,0:T(8,128)S(1)}, u32[]{:S(2)}, u32[]{:S(2)}) collective-permute-start(f32[16,2048]{1,0:T(8,128)S(1)} %collective-permute-done.1.refs_5_), channel_id=1, source_target_pairs={{0,7},{1,0},{2,1},{3,2},{4,3},{5,4},{6,5},{7,6},{8,15},{9,8},{10,9... | collective-permute-start | bytes 393224 | tf_op jit(solution)/shard_map/ppermute | solution.py:409
  15.9 8.5 %collective-permute-start.2 = (f32[16,2048]{1,0:T(8,128)S(1)}, f32[16,2048]{1,0:T(8,128)S(1)}, u32[]{:S(2)}, u32[]{:S(2)}) collective-permute-start(f32[16,2048]{1,0:T(8,128)S(1)} %collective-permute-done.refs_4_), channel_id=1, source_target_pairs={{0,1},{1,2},{2,3},{3,4},{4,5},{5,6},{6,7},{7,0},{8,9},{9,10},{10,1... | collective-permute-start | bytes 393224 | tf_op jit(solution)/shard_map/ppermute | solution.py:407
  21.5 8.9 %collective-permute-start.5 = (f32[16,2048]{1,0:T(8,128)S(1)}, f32[16,2048]{1,0:T(8,128)S(1)}, u32[]{:S(2)}, u32[]{:S(2)}) collective-permute-start(f32[16,2048]{1,0:T(8,128)S(1)} %collective-permute-done.3.refs_5_), channel_id=1, source_target_pairs={{0,7},{1,0},{2,1},{3,2},{4,3},{5,4},{6,5},{7,6},{8,15},{9,8},{10,9... | collective-permute-start | bytes 393224 | tf_op jit(solution)/shard_map/ppermute | solution.py:409
  24.4 5.6 %collective-permute-start.4 = (f32[16,2048]{1,0:T(8,128)S(1)}, f32[16,2048]{1,0:T(8,128)S(1)}, u32[]{:S(2)}, u32[]{:S(2)}) collective-permute-start(f32[16,2048]{1,0:T(8,128)S(1)} %collective-permute-done.2.refs_4_), channel_id=1, source_target_pairs={{0,1},{1,2},{2,3},{3,4},{4,5},{5,6},{6,7},{7,0},{8,9},{9,10},{10,1... | collective-permute-start | bytes 393224 | tf_op jit(solution)/shard_map/ppermute | solution.py:407
  30.0 5.9 %collective-permute-start.6 = (f32[16,2048]{1,0:T(8,128)S(1)}, f32[16,2048]{1,0:T(8,128)S(1)}, u32[]{:S(2)}, u32[]{:S(2)}) collective-permute-start(f32[16,2048]{1,0:T(8,128)S(1)} %collective-permute-done.4.refs_4_), channel_id=1, source_target_pairs={{0,1},{1,2},{2,3},{3,4},{4,5},{5,6},{6,7},{7,0},{8,9},{9,10},{10,1... | collective-permute-start | bytes 393224 | tf_op jit(solution)/shard_map/ppermute | solution.py:407
  89.7 21.4 %all-to-all-start.3 = ((f32[32,8,8,128]{3,2,1,0:T(8,128)}), f32[32,8,8,128]{3,2,1,0:T(8,128)S(1)}, u32[]{:S(2)}, u32[]{:S(2)}) async-start(f32[32,8,8,128]{3,2,1,0:T(8,128)} %get-tuple-element.12), calls=%async_computation.3 | async-start | bytes 2097152 | tf_op jit(solution)/shard_map/all_to_all | solution.py:392
  111.2 1.6 %copy-start.1 = (bf16[2048,512]{1,0:T(8,128)(2,1)S(1)}, bf16[2048,512]{1,0:T(8,128)(2,1)}, u32[]{:S(2)}) copy-start(bf16[2048,512]{1,0:T(8,128)(2,1)} %copy-done) | copy-start | bytes 6291460

commit v3 on v2

--- a/solution.py
+++ b/solution.py
@@ -45,13 +45,14 @@
 
 
 def dot_pieces(a, b, cb=0):
-    total = None
     n = len(a)
-    for i in reversed(range(n)):
-        for j in reversed(range(n - i)):
-            term = dot(a[i], b[j], 1, cb)
-            total = term if total is None else total + term
-    return total
+    pairs = [(i, j) for i in reversed(range(n)) for j in reversed(range(n - i))]
+    return dot(
+        jnp.concatenate([a[i] for i, _ in pairs], 1),
+        jnp.concatenate([b[j] for _, j in pairs], cb),
+        1,
+        cb,
+    )
 
 
 def select_frequencies(table_ref, seeds_ref, phases_ref):
@@ -184,13 +185,15 @@
         out_ref[k] = total
 
 
-def inverse_kernel(scale, packed_ref, inverse_ref, gram_ref):
+def inverse_kernel(scale, mine_ref, other_ref, inverse_ref, gram_ref):
     across = M // TILE
-    for r in range(packed_ref.shape[0]):
+    core = lax.axis_index("c")
+    for r in range(2 * mine_ref.shape[0]):
         i, j = divmod(r, across)
         for k in range(PANELS):
             first = 64 * panel_of(j, k) + 8 * i
-            gram_ref[first : first + 8, TILE * j : TILE * (j + 1)] = packed_ref[r, k] * scale
+            tile = jnp.where(core == r % 2, mine_ref[r // 2, k], other_ref[r // 2, k])
+            gram_ref[first : first + 8, TILE * j : TILE * (j + 1)] = tile * scale
     for i in range(across):
         j = (i + 1) % across
         lower = slice(TILE * i, TILE * (i + 1)), slice(TILE * j, TILE * (j + 1))
@@ -223,8 +226,8 @@
 
     lax.while_loop(more, step, error)
     x = inverse_ref[...]
-    rest = twice - dot_pieces(split3(gram_ref[...]), split3(x))
-    inverse_ref[...] = dot_pieces(split2(x), split2(rest))
+    rest = 0.5 * twice - dot_pieces(split3(gram_ref[...]), split3(x))
+    inverse_ref[...] = x + dot(x.astype(BF16), rest.astype(BF16))
 
 
 def finish_kernel(scale, inverse_ref, tiles, z_hbm, coef_ref, fitted_hbm, cross_ref, z, fitted, sems):
@@ -289,7 +292,7 @@
         kernel,
         in_specs=[HBM] * 5,
         out_specs=[VMEM, VMEM, VMEM, HBM],
-        out_shape=[shaped((112, M), BF16), shaped((wide, 112), BF16), shaped((cols + wide, M)), shaped((own, M), BF16)],
+        out_shape=[shaped((112, M), BF16), shaped((wide, 112), BF16), shaped((cols + wide, M)), pltpu.HBM((own, M), BF16)],
         scratch_shapes=[pltpu.VMEM(a.shape, a.dtype) for a in ins]
         + [pltpu.VMEM((own, M), BF16), pltpu.VMEM((cols + wide, own), BF16), pltpu.SemaphoreType.DMA((6,))],
         compiler_params=params(),
@@ -340,27 +343,27 @@
         pack_kernel,
         in_specs=[VMEM],
         out_specs=[VMEM, VMEM],
-        out_shape=[shaped((rows, PANELS, 8, TILE)), shaped((rows, parts.shape[0], 8, TILE))],
+        out_shape=[shaped((rows // 2, PANELS, 8, TILE)), shaped((rows, parts.shape[0], 8, TILE))],
         compiler_params=params(),
         cost_estimate=cost(1),
         name="packed",
     )(parts)
 
 
-def inverted(tiles, count):
+def inverted(mine, other, count):
     def kernel(*refs):
         inverse_kernel(1.0 / count, *refs)
 
     return pl.pallas_call(
         kernel,
-        in_specs=[VMEM],
+        in_specs=[VMEM, VMEM],
         out_specs=VMEM,
         out_shape=shaped((M, M)),
         scratch_shapes=[pltpu.VMEM((M, M), F32)],
         compiler_params=params(),
         cost_estimate=cost(16),
         name="inverted",
-    )(tiles)
+    )(mine, other)
 
 
 def finished(inverse, tiles, z, count):
@@ -385,7 +388,7 @@
         compiler_params=params(),
         cost_estimate=cost(4),
         name="finished",
-    )(inverse, tiles, z)
+    )(inverse, tiles, in_hbm(z))
 
 
 def exchanged(array, axes):
@@ -399,14 +402,14 @@
     x = samples.T
     t = treatment_features.T
 
-    ahead = [(k, (k + 1) % turn) for k in range(turn)]
-    back = [(k, (k - 1) % turn) for k in range(turn)]
-    right, left = [x], [x]
     half = turn // 2
-    for _ in range(half):
-        right.append(lax.ppermute(right[-1], "z", ahead))
-    for _ in range(half - 1):
-        left.append(lax.ppermute(left[-1], "z", back))
+
+    def moved(block, by):
+        return lax.ppermute(block, "z", [(k, (k + by) % turn) for k in range(turn)])
+
+    right = {1: moved(x, 1), 2: moved(x, 2)}
+    left = {1: moved(x, -1), 2: moved(x, -2)}
+    right[3], left[3], right[half] = moved(right[2], 1), moved(left[2], -1), moved(right[2], half - 2)
 
     freqs, panel, total, z = own_part(freq_table.T, feature_seeds[None, :], phases[None, :], x, t, turn)
     for k in range(1, half):
@@ -414,7 +417,8 @@
     total = more_part((-half,), freqs, panel, total, (right[half],), t, turn, tiled=True)
     parts = exchanged(spread(exchanged(total, ROWS), turn), "z")
     gram, cross = packed(parts, rows)
-    inverse = inverted(exchanged(gram, ROWS), count)
+    mine = exchanged(gram, ROWS[:2])
+    inverse = inverted(mine, lax.ppermute(mine, "c", [(0, 1), (1, 0)]), count)
     cross = exchanged(cross, ROWS)
     return finished(inverse, cross, z, count)
 

time: 118 us -> 112 us (0.949)
  blocking collectives: 49.8 us -> 41.1 us
  starting transfers between devices: 16.6 us -> 20.4 us
  local copies, waits for them, and re-layouts: 2.9 us -> 0 us
    all_to_all x3, blocking collectives: 49.8 us -> 41.1 us  [exchanged(): return lax.all_to_all(array, axes, 0, 0, tiled=True)]
    ppermute x7 -> x8, starting transfers between devices: 12.4 us -> 16.7 us  [the longest x7 13.7 us: moved(): return lax.ppermute(block, 'z', [(k, (k + by) % turn) for k in range(turn)])]
    unnamed x4 -> x0, local copies, waits for them, and re-layouts: 2.9 us -> none
  transfers between devices with their start and end apart: 8 -> 9, of which waited for: 1 -> 2; matrix products, arithmetic and copies ran while one was open for 0% -> 0% of each run, Pallas kernels for 29% -> 31%
where the time goes in v3:
time: 112 us; the launch traced here: 111 us
  Pallas kernels  43.9 us (39%)
  blocking collectives  41.1 us (37%)
  starting transfers between devices  20.4 us (18%)
  waiting for transfers between devices  4.91 us (4%)
    all_to_all x3, blocking collectives, exchanged(): return lax.all_to_all(array, axes, 0, 0, tiled=True)  41.1 us
    pallas_call x4, Pallas kernels, more_part(): pl.pallas_call(kernel, in_specs=[VMEM, VMEM, VMEM, HBM] + [VMEM] * n, out...  19.9 us
    ppermute x7, starting transfers between devices, moved(): return lax.ppermute(block, 'z', [(k, (k + by) % turn) for k in range(turn)])  13.7 us
    pallas_call x1, Pallas kernels, inverted(): pl.pallas_call(kernel, in_specs=[VMEM, VMEM], out_specs=VMEM, out_shape=s...  12.4 us
    pallas_call x1, Pallas kernels, own_part(): pl.pallas_call(kernel, in_specs=[HBM] * 5, out_specs=[VMEM, VMEM, VMEM, H...  5.41 us
    pallas_call x1, Pallas kernels, finished(): pl.pallas_call(kernel, in_specs=[VMEM, VMEM, HBM], out_specs=[VMEM, HBM],...  5.15 us
    all_to_all x1, waiting for transfers between devices, exchanged(): return lax.all_to_all(array, axes, 0, 0, tiled=True)  4.78 us
    all_to_all x1, starting transfers between devices, exchanged(): return lax.all_to_all(array, axes, 0, 0, tiled=True)  3.72 us
  transfers between devices with their start and end apart: 9, of which 2 were waited for; matrix products, arithmetic and copies ran while one was open for 0% of the time, Pallas kernels for 31%

profile of v3, /device:TPU:1, one launch (start us, length us, event | category | flops | bytes accessed | tf_op | source)
XLA Modules:
  0.0 111.2 jit_solution(3562935982244074286)
XLA Ops:
  0.6 6.9 %collective-permute-start.3 = (f32[16,2048]{1,0:T(8,128)}, f32[16,2048]{1,0:T(8,128)S(1)}, u32[]{:S(2)}, u32[]{:S(2)}) collective-permute-start(f32[16,2048]{1,0:T(8,128)} %bitcast.11), channel_id=1, source_target_pairs={{0,6},{1,7},{2,0},{3,1},{4,2},{5,3},{6,4},{7,5},{8,14},{9,15},{10,... | collective-permute-start | bytes 393224 | tf_op jit(solution)/shard_map/ppermute | solution.py:408
  7.6 0.0 collective-permute-start.2
  7.6 3.1 %collective-permute-start.1 = (f32[16,2048]{1,0:T(8,128)}, f32[16,2048]{1,0:T(8,128)S(1)}, u32[]{:S(2)}, u32[]{:S(2)}) collective-permute-start(f32[16,2048]{1,0:T(8,128)} %bitcast.13), channel_id=1, source_target_pairs={{0,7},{1,0},{2,1},{3,2},{4,3},{5,4},{6,5},{7,6},{8,15},{9,8},{10,9... | collective-permute-start | bytes 393224 | tf_op jit(solution)/shard_map/ppermute | solution.py:408
  10.7 0.0 collective-permute-start
  10.7 5.4 %own_part.1 = (bf16[112,512]{1,0:T(8,128)(2,1)S(1)}, bf16[64,112]{1,0:T(8,128)(2,1)S(1)}, f32[128,512]{1,0:T(8,128)S(1)}, bf16[2048,512]{1,0:T(8,128)(2,1)}) custom-call(f32[16,4096]{1,0:T(8,128)} %bitcast.10, s32[1,512]{1,0:T(1,128)} %bitcast.16, f32[1,512]{1,0:T(1,128)} %bitcast.17, f32[16,2048]{1,0:T(8,128)} %bitcast.15, bf16[64,16384]{1,0:T(8,128)(2,1)} %bitcast.5), custom_call_target="tpu_custom_call" | custom-call | flops 5750000128 | tf_op jit(solution)/shard_map/own_part/pallas_call | solution.py:291
  16.1 0.0 collective-permute-done.2.refs_4_
  16.1 0.1 collective-permute-start.6
  16.2 1.7 %collective-permute-start.4 = (f32[16,2048]{1,0:T(8,128)S(1)}, f32[16,2048]{1,0:T(8,128)S(1)}, u32[]{:S(2)}, u32[]{:S(2)}) collective-permute-start(f32[16,2048]{1,0:T(8,128)S(1)} %collective-permute-done.2.refs_4_), channel_id=1, source_target_pairs={{0,1},{1,2},{2,3},{3,4},{4,5},{5,6},{6,7},{7,0},{8,9},{9,10},{10,1... | collective-permute-start | bytes 393224 | tf_op jit(solution)/shard_map/ppermute | solution.py:408
  17.9 0.0 collective-permute-done.3.refs_5_
  17.9 1.8 %collective-permute-start.5 = (f32[16,2048]{1,0:T(8,128)S(1)}, f32[16,2048]{1,0:T(8,128)S(1)}, u32[]{:S(2)}, u32[]{:S(2)}) collective-permute-start(f32[16,2048]{1,0:T(8,128)S(1)} %collective-permute-done.3.refs_5_), channel_id=1, source_target_pairs={{0,7},{1,0},{2,1},{3,2},{4,3},{5,4},{6,5},{7,6},{8,15},{9,8},{10,9... | collective-permute-start | bytes 393224 | tf_op jit(solution)/shard_map/ppermute | solution.py:408
  19.7 0.0 collective-permute-done.1.refs_5_
  19.7 0.1 collective-permute-done.refs_4_
  19.8 5.6 %more_part.4.refs_2_ = f32[128,512]{1,0:T(8,128)S(1)} custom-call(bf16[112,512]{1,0:T(8,128)(2,1)S(1)} %get-tuple-element.8.refs_0_, bf16[64,112]{1,0:T(8,128)(2,1)S(1)} %get-tuple-element.9.refs_1_, f32[128,512]{1,0:T(8,128)S(1)} %get-tuple-element.10.refs_2_, bf16[64,16384]{1,0:T(8,128)(2,1)} %bitcast.6, f32[16,2048]{1,0:T(8,128)S(1)} %collective-permute-done.refs_4_, ...), custom_call_target="tpu_custom_call" | custom-call | flops 5980000256 | tf_op jit(solution)/shard_map/more_part/pallas_call | solution.py:313
  25.4 5.6 %more_part.5.refs_2_ = f32[128,512]{1,0:T(8,128)S(1)} custom-call(bf16[112,512]{1,0:T(8,128)(2,1)S(1)} %get-tuple-element.8.refs_0_, bf16[64,112]{1,0:T(8,128)(2,1)S(1)} %get-tuple-element.9.refs_1_, f32[128,512]{1,0:T(8,128)S(1)} %more_part.4.refs_2_, bf16[64,16384]{1,0:T(8,128)(2,1)} %bitcast.7, f32[16,2048]{1,0:T(8,128)S(1)} %collective-permute-done.2.refs_4_, ...), custom_call_target="tpu_custom_call" | custom-call | flops 5980000256 | tf_op jit(solution)/shard_map/more_part/pallas_call | solution.py:313
  31.0 0.0 collective-permute-done.5.refs_5_
  31.0 0.0 collective-permute-done.4.refs_4_
  31.1 5.8 %more_part.6.refs_2_ = f32[128,512]{1,0:T(8,128)S(1)} custom-call(bf16[112,512]{1,0:T(8,128)(2,1)S(1)} %get-tuple-element.8.refs_0_, bf16[64,112]{1,0:T(8,128)(2,1)S(1)} %get-tuple-element.9.refs_1_, f32[128,512]{1,0:T(8,128)S(1)} %more_part.5.refs_2_, bf16[64,16384]{1,0:T(8,128)(2,1)} %bitcast.8, f32[16,2048]{1,0:T(8,128)S(1)} %collective-permute-done.4.refs_4_, ...), custom_call_target="tpu_custom_call" | custom-call | flops 5980000256 | tf_op jit(solution)/shard_map/more_part/pallas_call | solution.py:313
  36.9 0.0 collective-permute-done.6.refs_4_
  36.9 2.9 %more_part.7 = f32[32,16,128]{2,1,0:T(8,128)S(1)} custom-call(bf16[112,512]{1,0:T(8,128)(2,1)S(1)} %get-tuple-element.8.refs_0_, bf16[64,112]{1,0:T(8,128)(2,1)S(1)} %get-tuple-element.9.refs_1_, f32[128,512]{1,0:T(8,128)S(1)} %more_part.6.refs_2_, bf16[64,16384]{1,0:T(8,128)(2,1)} %bitcast.9, f32[16,2048]{1,0:T(8,128)S(1)} %collective-permute-done.6.refs_4_), custom_call_target="tpu_custom_call" | custom-call | flops 2990000128 | tf_op jit(solution)/shard_map/more_part/pallas_call | solution.py:313
  39.8 18.7 %all_to_all.20.parts = f32[32,16,128]{2,1,0:T(8,128)S(1)} all-to-all(f32[32,16,128]{2,1,0:T(8,128)S(1)} %more_part.7), channel_id=1, replica_groups=mesh['y'=4,'x'=4,'c'=2,'z'=8] {'y','x','c'}, dimensions={0} | all-to-all | bytes 524288 | tf_op jit(solution)/shard_map/all_to_all | solution.py:395
  58.5 11.1 %all_to_all.21.parts_ref = f32[8,16,128]{2,1,0:T(8,128)S(1)} all-to-all(f32[8,16,128]{2,1,0:T(8,128)S(1)} %spread.1), channel_id=1, replica_groups=mesh['y'=4,'x'=4,'c'=2,'z'=8] {'z'}, dimensions={0} | all-to-all | bytes 131072 | tf_op jit(solution)/shard_map/all_to_all | solution.py:395
  69.6 1.1 packed.1
  70.7 11.3 %all_to_all.22.refs_0_ = f32[16,6,8,128]{3,2,1,0:T(8,128)S(1)} all-to-all(f32[16,6,8,128]{3,2,1,0:T(8,128)S(1)} %get-tuple-element.11), channel_id=1, replica_groups=mesh['y'=4,'x'=4,'c'=2,'z'=8] {'y','x'}, dimensions={0} | all-to-all | bytes 786432 | tf_op jit(solution)/shard_map/all_to_all | solution.py:395
  82.0 3.0 %collective-permute-start.7 = (f32[16,6,8,128]{3,2,1,0:T(8,128)S(1)}, f32[16,6,8,128]{3,2,1,0:T(8,128)S(1)}, u32[]{:S(2)}, u32[]{:S(2)}) collective-permute-start(f32[16,6,8,128]{3,2,1,0:T(8,128)S(1)} %all_to_all.22.refs_0_), channel_id=1, source_target_pairs={{0,8},{8,0},{1,9},{9,1},{2,10},{10,2},{3,11},{11,3},{4,12},{12,4},... | collective-permute-start | bytes 1179656 | tf_op jit(solution)/shard_map/ppermute | solution.py:421
  85.0 3.7 %all-to-all-start.3 = ((f32[32,8,8,128]{3,2,1,0:T(8,128)}), f32[32,8,8,128]{3,2,1,0:T(8,128)S(1)}, u32[]{:S(2)}, u32[]{:S(2)}) async-start(f32[32,8,8,128]{3,2,1,0:T(8,128)} %get-tuple-element.12), calls=%async_computation.3 | async-start | bytes 2097152 | tf_op jit(solution)/shard_map/all_to_all | solution.py:395
  88.7 0.0 collective-permute-done.7.refs_1_
  88.7 12.4 %inverted.1.refs_0_ = f32[512,512]{1,0:T(8,128)S(1)} custom-call(f32[16,6,8,128]{3,2,1,0:T(8,128)S(1)} %all_to_all.22.refs_0_, f32[16,6,8,128]{3,2,1,0:T(8,128)S(1)} %collective-permute-done.7.refs_1_), custom_call_target="tpu_custom_call" | custom-call | flops 18400000000 | tf_op jit(solution)/shard_map/inverted/pallas_call | solution.py:357
  101.1 4.8 %all-to-all-done.3.refs_1_ = f32[32,8,8,128]{3,2,1,0:T(8,128)S(1)} async-done(((f32[32,8,8,128]{3,2,1,0:T(8,128)}), f32[32,8,8,128]{3,2,1,0:T(8,128)S(1)}, u32[]{:S(2)}, u32[]{:S(2)}) %all-to-all-start.3) | async-done | bytes 1048608 | tf_op jit(solution)/shard_map/all_to_all | solution.py:395
  105.9 5.2 %finished.1 = (f32[512,512]{1,0:T(8,128)}, f32[2048,512]{1,0:T(8,128)}) custom-call(f32[512,512]{1,0:T(8,128)S(1)} %inverted.1.refs_0_, f32[32,8,8,128]{3,2,1,0:T(8,128)S(1)} %all-to-all-done.3.refs_1_, bf16[2048,512]{1,0:T(8,128)(2,1)} %get-tuple-element.13.refs_2_), custom_call_target="tpu_custom_call" | custom-call | flops 4600000000 | tf_op jit(solution)/shard_map/finished/pallas_call | solution.py:377
  (1 shorter events, 0.0 us)
Async XLA Ops:
  0.6 17.3 %collective-permute-start.3 = (f32[16,2048]{1,0:T(8,128)}, f32[16,2048]{1,0:T(8,128)S(1)}, u32[]{:S(2)}, u32[]{:S(2)}) collective-permute-start(f32[16,2048]{1,0:T(8,128)} %bitcast.11), channel_id=1, source_target_pairs={{0,6},{1,7},{2,0},{3,1},{4,2},{5,3},{6,4},{7,5},{8,14},{9,15},{10,... | collective-permute-start | bytes 393224 | tf_op jit(solution)/shard_map/ppermute | solution.py:408
  7.6 8.6 %collective-permute-start.2 = (f32[16,2048]{1,0:T(8,128)}, f32[16,2048]{1,0:T(8,128)S(1)}, u32[]{:S(2)}, u32[]{:S(2)}) collective-permute-start(f32[16,2048]{1,0:T(8,128)} %bitcast.12), channel_id=1, source_target_pairs={{0,2},{1,3},{2,4},{3,5},{4,6},{5,7},{6,0},{7,1},{8,10},{9,11},{10,... | collective-permute-start | bytes 393224 | tf_op jit(solution)/shard_map/ppermute | solution.py:408
  7.6 12.2 %collective-permute-start.1 = (f32[16,2048]{1,0:T(8,128)}, f32[16,2048]{1,0:T(8,128)S(1)}, u32[]{:S(2)}, u32[]{:S(2)}) collective-permute-start(f32[16,2048]{1,0:T(8,128)} %bitcast.13), channel_id=1, source_target_pairs={{0,7},{1,0},{2,1},{3,2},{4,3},{5,4},{6,5},{7,6},{8,15},{9,8},{10,9... | collective-permute-start | bytes 393224 | tf_op jit(solution)/shard_map/ppermute | solution.py:408
  10.7 9.1 %collective-permute-start = (f32[16,2048]{1,0:T(8,128)}, f32[16,2048]{1,0:T(8,128)S(1)}, u32[]{:S(2)}, u32[]{:S(2)}) collective-permute-start(f32[16,2048]{1,0:T(8,128)} %bitcast.14), channel_id=1, source_target_pairs={{0,1},{1,2},{2,3},{3,4},{4,5},{5,6},{6,7},{7,0},{8,9},{9,10},{10,1... | collective-permute-start | bytes 393224 | tf_op jit(solution)/shard_map/ppermute | solution.py:408
  16.1 20.8 %collective-permute-start.6 = (f32[16,2048]{1,0:T(8,128)S(1)}, f32[16,2048]{1,0:T(8,128)S(1)}, u32[]{:S(2)}, u32[]{:S(2)}) collective-permute-start(f32[16,2048]{1,0:T(8,128)S(1)} %collective-permute-done.2.refs_4_), channel_id=1, source_target_pairs={{0,2},{1,3},{2,4},{3,5},{4,6},{5,7},{6,0},{7,1},{8,10},{9,11},{10,... | collective-permute-start | bytes 393224 | tf_op jit(solution)/shard_map/ppermute | solution.py:408
  16.2 14.8 %collective-permute-start.4 = (f32[16,2048]{1,0:T(8,128)S(1)}, f32[16,2048]{1,0:T(8,128)S(1)}, u32[]{:S(2)}, u32[]{:S(2)}) collective-permute-start(f32[16,2048]{1,0:T(8,128)S(1)} %collective-permute-done.2.refs_4_), channel_id=1, source_target_pairs={{0,1},{1,2},{2,3},{3,4},{4,5},{5,6},{6,7},{7,0},{8,9},{9,10},{10,1... | collective-permute-start | bytes 393224 | tf_op jit(solution)/shard_map/ppermute | solution.py:408
  17.9 13.1 %collective-permute-start.5 = (f32[16,2048]{1,0:T(8,128)S(1)}, f32[16,2048]{1,0:T(8,128)S(1)}, u32[]{:S(2)}, u32[]{:S(2)}) collective-permute-start(f32[16,2048]{1,0:T(8,128)S(1)} %collective-permute-done.3.refs_5_), channel_id=1, source_target_pairs={{0,7},{1,0},{2,1},{3,2},{4,3},{5,4},{6,5},{7,6},{8,15},{9,8},{10,9... | collective-permute-start | bytes 393224 | tf_op jit(solution)/shard_map/ppermute | solution.py:408
  82.0 6.7 %collective-permute-start.7 = (f32[16,6,8,128]{3,2,1,0:T(8,128)S(1)}, f32[16,6,8,128]{3,2,1,0:T(8,128)S(1)}, u32[]{:S(2)}, u32[]{:S(2)}) collective-permute-start(f32[16,6,8,128]{3,2,1,0:T(8,128)S(1)} %all_to_all.22.refs_0_), channel_id=1, source_target_pairs={{0,8},{8,0},{1,9},{9,1},{2,10},{10,2},{3,11},{11,3},{4,12},{12,4},... | collective-permute-start | bytes 1179656 | tf_op jit(solution)/shard_map/ppermute | solution.py:421
  85.0 20.9 %all-to-all-start.3 = ((f32[32,8,8,128]{3,2,1,0:T(8,128)}), f32[32,8,8,128]{3,2,1,0:T(8,128)S(1)}, u32[]{:S(2)}, u32[]{:S(2)}) async-start(f32[32,8,8,128]{3,2,1,0:T(8,128)} %get-tuple-element.12), calls=%async_computation.3 | async-start | bytes 2097152 | tf_op jit(solution)/shard_map/all_to_all | solution.py:395

commit v4 on v3

--- a/solution.py
+++ b/solution.py
@@ -20,7 +20,7 @@
 
 def sine_coefficients():
     nodes = 0.25 * np.cos(np.pi * (np.arange(400) + 0.5) / 800)
-    powers = np.stack([nodes ** (2 * k + 1) for k in range(5)], 1)
+    powers = np.stack([nodes ** (2 * k + 1) for k in range(4)], 1)
     return [float(c) for c in np.linalg.lstsq(powers, np.sqrt(2) * np.sin(2 * np.pi * nodes), rcond=None)[0]]
 
 
@@ -53,6 +53,13 @@
         1,
         cb,
     )
+
+
+def mirrored_product(a, b):
+    half = a[0].shape[0] // 2
+    upper = dot_pieces([p[:half] for p in a], [p[:, :half] for p in b])
+    lower = dot_pieces([p[half:] for p in a], b)
+    return jnp.concatenate([jnp.concatenate([upper, lower[:, :half].T], 1), lower], 0)
 
 
 def select_frequencies(table_ref, seeds_ref, phases_ref):
@@ -84,8 +91,8 @@
     angle = angle - jnp.round(angle)
     q = 0.25 - jnp.abs(angle)
     s = q * q
-    p = COEFFS[4] * s + COEFFS[3]
-    for c in COEFFS[2::-1]:
+    p = COEFFS[3] * s + COEFFS[2]
+    for c in COEFFS[1::-1]:
         p = p * s + c
     return (p * q).astype(BF16)
 
@@ -185,7 +192,8 @@
         out_ref[k] = total
 
 
-def inverse_kernel(scale, mine_ref, other_ref, inverse_ref, gram_ref):
+def inverse_kernel(scale, mine_ref, other_ref, gram_ref, inverse_ref, error_ref, scale_ref):
+    scale_ref[...] = jnp.full(scale_ref.shape, scale, F32)
     across = M // TILE
     core = lax.axis_index("c")
     for r in range(2 * mine_ref.shape[0]):
@@ -198,50 +206,81 @@
         j = (i + 1) % across
         lower = slice(TILE * i, TILE * (i + 1)), slice(TILE * j, TILE * (j + 1))
         gram_ref[lower] = gram_ref[lower[::-1]].T
+    eye = identity()
+    gram = gram_ref[...] + RIDGE * eye
+    gram_ref[...] = gram
+    g = split2(gram)
+    square = mirrored_product(g, g)
+
+    def bound(matrix):
+        return jnp.max(jnp.sum(jnp.abs(matrix), axis=0, keepdims=True), axis=1, keepdims=True)
+
+    top = jnp.minimum(bound(gram), jnp.sqrt(bound(square)) * 1.0001)
+    low = jnp.full((1, 1), RIDGE * 0.999, F32)
+    m, c = 2.0 / (top - low), (top + low) / (top - low)
+    c2, c3, c4 = c * c, c * c * c, c * c * c * c
+    last = 16.0 * c4 * c - 20.0 * c3 + 5.0 * c
+    p = (
+        (80.0 * c4 - 60.0 * c2 + 5.0) * m / last,
+        (60.0 * c - 160.0 * c3) * m * m / last,
+        (160.0 * c2 - 20.0) * m * m * m / last,
+        -80.0 * c * m * m * m * m / last,
+        16.0 * m * m * m * m * m / last,
+    )
+    factor = p[2] * eye + p[3] * gram + p[4] * square
+    inverse_ref[...] = p[0] * eye + p[1] * gram + mirrored_product(split2(square), split2(factor))
+    error = improved(inverse_ref, g, 1.0 / last, 0.15)
+    error_ref[...] = jnp.broadcast_to(error, error_ref.shape)
+
+
+def identity():
     line = lax.broadcasted_iota(jnp.int32, (M, M), 0)
     lane = lax.broadcasted_iota(jnp.int32, (M, M), 1)
-    twice = jnp.where(line == lane, F32(2), F32(0))
-    gram = gram_ref[...] + (RIDGE / 2) * twice
-    gram_ref[...] = gram
-    sums = jnp.sum(jnp.abs(gram), axis=0, keepdims=True)
-    top = jnp.max(sums, axis=1, keepdims=True)
-    low = jnp.full((1, 1), RIDGE * 0.999, F32)
-    first = 2.0 / (top + low)
-    error = (top - low) / (top + low)
-    gain = 2.0 / (2.0 - error * error)
-    inverse_ref[...] = (gain * first) * (twice - first * gram)
-    error = error * error * 0.5 * gain
-    g = split2(gram)
-
-    def more(state):
-        return jnp.max(state) > 2e-3
+    return jnp.where(line == lane, F32(1), F32(0))
+
+
+def improved(inverse_ref, g, error, goal):
+    twice = 2.0 * identity()
+
+    def more(error):
+        return jnp.max(error) > goal
 
     def step(error):
         gain = 2.0 / (2.0 - error * error)
-        x = inverse_ref[...]
-        pieces = split2(x)
+        pieces = split2(inverse_ref[...])
         rest = twice - dot_pieces(g, pieces)
-        inverse_ref[...] = gain * dot_pieces(pieces, split2(rest))
+        inverse_ref[...] = gain * mirrored_product(pieces, split2(rest))
         return error * error * 0.5 * gain
 
-    lax.while_loop(more, step, error)
+    return lax.while_loop(more, step, error)
+
+
+def polish_kernel(after_ref, gram_ref, start_ref, error_ref, inverse_ref):
+    gram = gram_ref[...]
+    inverse_ref[...] = start_ref[...]
+    improved(inverse_ref, split2(gram), error_ref[:1, :1], 1e-2)
     x = inverse_ref[...]
-    rest = 0.5 * twice - dot_pieces(split3(gram_ref[...]), split3(x))
-    inverse_ref[...] = x + dot(x.astype(BF16), rest.astype(BF16))
-
-
-def finish_kernel(scale, inverse_ref, tiles, z_hbm, coef_ref, fitted_hbm, cross_ref, z, fitted, sems):
+    rest = identity() - dot_pieces(split3(gram), split3(x))
+    low = rest.astype(BF16)
+    rest = rest + dot(low, low)
+    inverse_ref[...] = x + dot_pieces(split2(x), split2(rest))
+
+
+def finish_kernel(inverse_ref, mine_ref, other_ref, z_hbm, coef_ref, fitted_hbm, cross_ref, z, fitted, sems):
     n = z.shape[0]
     lines = z.shape[1]
     spans = [pl.ds(k * lines, lines) for k in range(n)]
     copies = copied([(z_hbm.at[span], z.at[k]) for k, span in enumerate(spans)], sems)
     x = split2(inverse_ref[...])
     across = M // TILE
-    for r in range(tiles.shape[0]):
+    core = lax.axis_index("c")
+    turn = mine_ref.shape[1]
+    for r in range(2 * mine_ref.shape[0]):
         i, j = divmod(r, across)
-        for k in range(tiles.shape[1]):
-            first = k * (M // tiles.shape[1]) + 8 * i
-            cross_ref[first : first + 8, TILE * j : TILE * (j + 1)] = tiles[r, k] * scale
+        for k in range(turn):
+            first = k * (M // turn) + 8 * i
+            tile = jnp.where(core == r % 2, mine_ref[r // 2, k], other_ref[r // 2, k])
+            cross_ref[first : first + 8, TILE * j : TILE * (j + 1)] = tile
     coef = dot_pieces(x, split2(cross_ref[...]), 1)
     coef_ref[...] = coef
     low = coef.astype(BF16)
@@ -343,7 +382,7 @@
         pack_kernel,
         in_specs=[VMEM],
         out_specs=[VMEM, VMEM],
-        out_shape=[shaped((rows // 2, PANELS, 8, TILE)), shaped((rows, parts.shape[0], 8, TILE))],
+        out_shape=[shaped((rows // 2, PANELS, 8, TILE)), shaped((rows // 2, parts.shape[0], 8, TILE))],
         compiler_params=params(),
         cost_estimate=cost(1),
         name="packed",
@@ -357,26 +396,34 @@
     return pl.pallas_call(
         kernel,
         in_specs=[VMEM, VMEM],
+        out_specs=[VMEM] * 4,
+        out_shape=[shaped((M, M)), shaped((M, M)), shaped((8, TILE)), shaped((8, TILE))],
+        compiler_params=params(),
+        cost_estimate=cost(9),
+        name="inverted",
+    )(mine, other)
+
+
+def polished(after, gram, start, error):
+    return pl.pallas_call(
+        polish_kernel,
+        in_specs=[pl.BlockSpec(memory_space=pl.ANY)] + [VMEM] * 3,
         out_specs=VMEM,
         out_shape=shaped((M, M)),
-        scratch_shapes=[pltpu.VMEM((M, M), F32)],
-        compiler_params=params(),
-        cost_estimate=cost(16),
-        name="inverted",
-    )(mine, other)
-
-
-def finished(inverse, tiles, z, count):
+        compiler_params=params(),
+        cost_estimate=cost(5),
+        name="polished",
+    )(after, gram, start, error)
+
+
+def finished(inverse, mine, other, z):
     own = z.shape[0]
     n = 4
     lines = own // n
 
-    def kernel(*refs):
-        finish_kernel(1.0 / count, *refs)
-
-    return pl.pallas_call(
-        kernel,
-        in_specs=[VMEM, VMEM, HBM],
+    return pl.pallas_call(
+        finish_kernel,
+        in_specs=[VMEM, VMEM, VMEM, HBM],
         out_specs=[VMEM, HBM],
         out_shape=[shaped((M, M)), shaped((own, M))],
         scratch_shapes=[
@@ -388,7 +435,7 @@
         compiler_params=params(),
         cost_estimate=cost(4),
         name="finished",
-    )(inverse, tiles, in_hbm(z))
+    )(inverse, mine, other, in_hbm(z))
 
 
 def exchanged(array, axes):
@@ -412,15 +459,21 @@
     right[3], left[3], right[half] = moved(right[2], 1), moved(left[2], -1), moved(right[2], half - 2)
 
     freqs, panel, total, z = own_part(freq_table.T, feature_seeds[None, :], phases[None, :], x, t, turn)
-    for k in range(1, half):
-        total = more_part((-k, k), freqs, panel, total, (right[k], left[k]), t, turn)
-    total = more_part((-half,), freqs, panel, total, (right[half],), t, turn, tiled=True)
+    near = (right[1], left[1], right[2], left[2])
+    total = more_part((-1, 1, -2, 2), freqs, panel, total, near, t, turn)
+    far = (right[3], left[3], right[half])
+    total = more_part((-3, 3, -half), freqs, panel, total, far, t, turn, tiled=True)
     parts = exchanged(spread(exchanged(total, ROWS), turn), "z")
     gram, cross = packed(parts, rows)
-    mine = exchanged(gram, ROWS[:2])
-    inverse = inverted(mine, lax.ppermute(mine, "c", [(0, 1), (1, 0)]), count)
-    cross = exchanged(cross, ROWS)
-    return finished(inverse, cross, z, count)
+    gram = exchanged(gram, ROWS[:2])
+    *start, scale = inverted(gram, swapped(gram), count)
+    cross = exchanged(cross, ROWS[:2]) * scale
+    inverse = polished(cross, *start)
+    return finished(inverse, cross, swapped(cross), z)
+
+
+def swapped(array):
+    return lax.ppermute(array, "c", [(0, 1), (1, 0)])
 
 
 def solution(mesh):

time: 112 us -> 109 us (0.973)
  Pallas kernels: 43.9 us -> 39.7 us
  starting transfers between devices: 20.4 us -> 21.7 us
    pallas_call x4 -> x2, Pallas kernels: 19.9 us -> 17.2 us  [more_part(): pl.pallas_call(kernel, in_specs=[VMEM, VMEM, VMEM, HBM] + [VMEM] * n, out...]
    ppermute x1 -> x2, starting transfers between devices: 2.99 us -> 4.16 us  [swapped(): return lax.ppermute(array, 'c', [(0, 1), (1, 0)])]
    pallas_call x2 -> x3, Pallas kernels: 17.5 us -> 16.5 us  [the longest x1 5.93 us: inverted(): pl.pallas_call(kernel, in_specs=[VMEM, VMEM], out_specs=[VMEM] * 4, out_s...]
  transfers between devices with their start and end apart: 9 -> 10, of which waited for: 2 -> 2; matrix products, arithmetic and copies ran while one was open for 0% -> 0% of each run, Pallas kernels for 31% -> 24%
where the time goes in v4:
time: 109 us
  blocking collectives  40.8 us (37%)
  Pallas kernels  39.7 us (36%)
  starting transfers between devices  21.7 us (20%)
  waiting for transfers between devices  5.55 us (5%)
    all_to_all x3, blocking collectives, exchanged(): return lax.all_to_all(array, axes, 0, 0, tiled=True)  40.8 us
    pallas_call x2, Pallas kernels, more_part(): pl.pallas_call(kernel, in_specs=[VMEM, VMEM, VMEM, HBM] + [VMEM] * n, out...  17.2 us
    ppermute x7, starting transfers between devices, moved(): return lax.ppermute(block, 'z', [(k, (k + by) % turn) for k in range(turn)])  14 us
    pallas_call x1, Pallas kernels, inverted(): pl.pallas_call(kernel, in_specs=[VMEM, VMEM], out_specs=[VMEM] * 4, out_s...  5.93 us
    all_to_all x1, waiting for transfers between devices, exchanged(): return lax.all_to_all(array, axes, 0, 0, tiled=True)  5.42 us
    pallas_call x1, Pallas kernels, polished(): pl.pallas_call(polish_kernel, in_specs=[pl.BlockSpec(memory_space=pl.ANY)...  5.4 us
    pallas_call x1, Pallas kernels, finished(): pl.pallas_call(finish_kernel, in_specs=[VMEM, VMEM, VMEM, HBM], out_specs...  5.17 us
    pallas_call x1, Pallas kernels, own_part(): pl.pallas_call(kernel, in_specs=[HBM] * 5, out_specs=[VMEM, VMEM, VMEM, H...  5.09 us
  transfers between devices with their start and end apart: 10, of which 2 were waited for; matrix products, arithmetic and copies ran while one was open for 0% of the time, Pallas kernels for 24%

profile of v4, /device:TPU:1, one launch (start us, length us, event | category | flops | bytes accessed | tf_op | source)
XLA Modules:
  0.0 108.7 jit_solution(7354336199322831820)
XLA Ops:
  0.6 6.9 %collective-permute-start.3 = (f32[16,2048]{1,0:T(8,128)}, f32[16,2048]{1,0:T(8,128)S(1)}, u32[]{:S(2)}, u32[]{:S(2)}) collective-permute-start(f32[16,2048]{1,0:T(8,128)} %bitcast.9), channel_id=1, source_target_pairs={{0,6},{1,7},{2,0},{3,1},{4,2},{5,3},{6,4},{7,5},{8,14},{9,15},{10,... | collective-permute-start | bytes 393224 | tf_op jit(solution)/shard_map/ppermute | solution.py:455
  7.6 0.0 collective-permute-start.2
  7.6 3.1 %collective-permute-start.1 = (f32[16,2048]{1,0:T(8,128)}, f32[16,2048]{1,0:T(8,128)S(1)}, u32[]{:S(2)}, u32[]{:S(2)}) collective-permute-start(f32[16,2048]{1,0:T(8,128)} %bitcast.11), channel_id=1, source_target_pairs={{0,7},{1,0},{2,1},{3,2},{4,3},{5,4},{6,5},{7,6},{8,15},{9,8},{10,9... | collective-permute-start | bytes 393224 | tf_op jit(solution)/shard_map/ppermute | solution.py:455
  10.7 0.0 collective-permute-start
  10.7 5.1 %own_part.1 = (bf16[112,512]{1,0:T(8,128)(2,1)S(1)}, bf16[64,112]{1,0:T(8,128)(2,1)S(1)}, f32[128,512]{1,0:T(8,128)S(1)}, bf16[2048,512]{1,0:T(8,128)(2,1)}) custom-call(f32[16,4096]{1,0:T(8,128)} %bitcast.8, s32[1,512]{1,0:T(1,128)} %bitcast.14, f32[1,512]{1,0:T(1,128)} %bitcast.15, f32[16,2048]{1,0:T(8,128)} %bitcast.13, bf16[64,16384]{1,0:T(8,128)(2,1)} %bitcast.5), custom_call_target="tpu_custom_call" | custom-call | flops 5750000128 | tf_op jit(solution)/shard_map/own_part/pallas_call | solution.py:330
  15.8 0.0 collective-permute-done.2.refs_6_
  15.8 0.1 collective-permute-start.6
  15.9 1.7 %collective-permute-start.4 = (f32[16,2048]{1,0:T(8,128)S(1)}, f32[16,2048]{1,0:T(8,128)S(1)}, u32[]{:S(2)}, u32[]{:S(2)}) collective-permute-start(f32[16,2048]{1,0:T(8,128)S(1)} %collective-permute-done.2.refs_6_), channel_id=1, source_target_pairs={{0,1},{1,2},{2,3},{3,4},{4,5},{5,6},{6,7},{7,0},{8,9},{9,10},{10,1... | collective-permute-start | bytes 393224 | tf_op jit(solution)/shard_map/ppermute | solution.py:455
  17.6 0.0 collective-permute-done.3.refs_7_
  17.6 2.1 %collective-permute-start.5 = (f32[16,2048]{1,0:T(8,128)S(1)}, f32[16,2048]{1,0:T(8,128)S(1)}, u32[]{:S(2)}, u32[]{:S(2)}) collective-permute-start(f32[16,2048]{1,0:T(8,128)S(1)} %collective-permute-done.3.refs_7_), channel_id=1, source_target_pairs={{0,7},{1,0},{2,1},{3,2},{4,3},{5,4},{6,5},{7,6},{8,15},{9,8},{10,9... | collective-permute-start | bytes 393224 | tf_op jit(solution)/shard_map/ppermute | solution.py:455
  19.7 0.0 collective-permute-done.1.refs_5_
  19.7 0.1 collective-permute-done.refs_4_
  19.8 9.7 %more_part.2.refs_2_ = f32[128,512]{1,0:T(8,128)S(1)} custom-call(bf16[112,512]{1,0:T(8,128)(2,1)S(1)} %get-tuple-element.12.refs_0_, bf16[64,112]{1,0:T(8,128)(2,1)S(1)} %get-tuple-element.13.refs_1_, f32[128,512]{1,0:T(8,128)S(1)} %get-tuple-element.14.refs_2_, bf16[64,16384]{1,0:T(8,128)(2,1)} %bitcast.6, f32[16,2048]{1,0:T(8,128)S(1)} %collective-permute-done.refs_4_, ...), custom_call_target="tpu_custom_call" | custom-call | flops 11960000512 | tf_op jit(solution)/shard_map/more_part/pallas_call | solution.py:352
  29.5 0.0 collective-permute-done.5.refs_5_
  29.6 0.0 collective-permute-done.6.refs_6_
  29.6 0.0 collective-permute-done.4.refs_4_
  29.6 7.5 %more_part.3 = f32[32,16,128]{2,1,0:T(8,128)S(1)} custom-call(bf16[112,512]{1,0:T(8,128)(2,1)S(1)} %get-tuple-element.12.refs_0_, bf16[64,112]{1,0:T(8,128)(2,1)S(1)} %get-tuple-element.13.refs_1_, f32[128,512]{1,0:T(8,128)S(1)} %more_part.2.refs_2_, bf16[64,16384]{1,0:T(8,128)(2,1)} %bitcast.7, f32[16,2048]{1,0:T(8,128)S(1)} %collective-permute-done.4.refs_4_, ...), custom_call_target="tpu_custom_call" | custom-call | flops 8970000384 | tf_op jit(solution)/shard_map/more_part/pallas_call | solution.py:352
  37.1 18.7 %all_to_all.20.parts = f32[32,16,128]{2,1,0:T(8,128)S(1)} all-to-all(f32[32,16,128]{2,1,0:T(8,128)S(1)} %more_part.3), channel_id=1, replica_groups=mesh['y'=4,'x'=4,'c'=2,'z'=8] {'y','x','c'}, dimensions={0} | all-to-all | bytes 524288 | tf_op jit(solution)/shard_map/all_to_all | solution.py:442
  55.8 10.7 %all_to_all.21.parts_ref = f32[8,16,128]{2,1,0:T(8,128)S(1)} all-to-all(f32[8,16,128]{2,1,0:T(8,128)S(1)} %spread.1), channel_id=1, replica_groups=mesh['y'=4,'x'=4,'c'=2,'z'=8] {'z'}, dimensions={0} | all-to-all | bytes 131072 | tf_op jit(solution)/shard_map/all_to_all | solution.py:442
  66.6 0.8 packed.1
  67.4 11.3 %all_to_all.22.refs_0_ = f32[16,6,8,128]{3,2,1,0:T(8,128)S(1)} all-to-all(f32[16,6,8,128]{3,2,1,0:T(8,128)S(1)} %get-tuple-element.16), channel_id=1, replica_groups=mesh['y'=4,'x'=4,'c'=2,'z'=8] {'y','x'}, dimensions={0} | all-to-all | bytes 786432 | tf_op jit(solution)/shard_map/all_to_all | solution.py:442
  78.8 3.0 %collective-permute-start.7 = (f32[16,6,8,128]{3,2,1,0:T(8,128)S(1)}, f32[16,6,8,128]{3,2,1,0:T(8,128)S(1)}, u32[]{:S(2)}, u32[]{:S(2)}) collective-permute-start(f32[16,6,8,128]{3,2,1,0:T(8,128)S(1)} %all_to_all.22.refs_0_), channel_id=1, source_target_pairs={{0,8},{8,0},{1,9},{9,1},{2,10},{10,2},{3,11},{11,3},{4,12},{12,4},... | collective-permute-start | bytes 1179656 | tf_op jit(solution)/shard_map/ppermute | solution.py:476
  81.8 3.6 %all-to-all-start.2 = ((f32[16,8,8,128]{3,2,1,0:T(8,128)}), f32[16,8,8,128]{3,2,1,0:T(8,128)S(1)}, u32[]{:S(2)}, u32[]{:S(2)}) async-start(f32[16,8,8,128]{3,2,1,0:T(8,128)} %get-tuple-element.15), calls=%async_computation.2 | async-start | bytes 1048576 | tf_op jit(solution)/shard_map/all_to_all | solution.py:442
  85.3 0.0 collective-permute-done.7.refs_1_
  85.4 5.9 %inverted.1 = (f32[512,512]{1,0:T(8,128)S(1)}, f32[512,512]{1,0:T(8,128)S(1)}, f32[8,128]{1,0:T(8,128)S(1)}, f32[8,128]{1,0:T(8,128)S(1)}) custom-call(f32[16,6,8,128]{3,2,1,0:T(8,128)S(1)} %all_to_all.22.refs_0_, f32[16,6,8,128]{3,2,1,0:T(8,128)S(1)} %collective-permute-done.7.refs_1_), custom_call_target="tpu_custom_call" | custom-call | flops 10350000128 | tf_op jit(solution)/shard_map/inverted/pallas_call | solution.py:396
  91.3 5.4 %all-to-all-done.2 = f32[16,8,8,128]{3,2,1,0:T(8,128)S(1)} async-done(((f32[16,8,8,128]{3,2,1,0:T(8,128)}), f32[16,8,8,128]{3,2,1,0:T(8,128)S(1)}, u32[]{:S(2)}, u32[]{:S(2)}) %all-to-all-start.2) | async-done | bytes 524320 | tf_op jit(solution)/shard_map/all_to_all | solution.py:442
  96.8 1.2 %collective-permute-start.8 = (f32[16,8,8,128]{3,2,1,0:T(8,128)S(1)}, f32[16,8,8,128]{3,2,1,0:T(8,128)S(1)}, u32[]{:S(2)}, u32[]{:S(2)}) collective-permute-start(f32[16,8,8,128]{3,2,1,0:T(8,128)S(1)} %broadcast_multiply_fusion.after_ref.mine_ref), channel_id=1, source_target_pairs={{0,8},{8,0},{1,9},{9,1},{2,10},{10,2},{3,11},{11,3},{4,12},{12,4},... | collective-permute-start | bytes 1572872 | tf_op jit(solution)/shard_map/ppermute | solution.py:476
  97.9 5.4 %polished.1.inverse_ref = f32[512,512]{1,0:T(8,128)S(1)} custom-call(f32[16,8,8,128]{3,2,1,0:T(8,128)S(1)} %broadcast_multiply_fusion.after_ref.mine_ref, f32[512,512]{1,0:T(8,128)S(1)} %get-tuple-element.18.gram_ref, f32[512,512]{1,0:T(8,128)S(1)} %get-tuple-element.19.start_ref, f32[8,128]{1,0:T(8,128)S(1)} %get-tuple-element.20.error_ref), custom_call_target="tpu_custom_call" | custom-call | flops 5750000128 | tf_op jit(solution)/shard_map/polished/pallas_call | solution.py:408
  103.3 0.0 collective-permute-done.8.other_ref
  103.3 5.2 %finished.1 = (f32[512,512]{1,0:T(8,128)}, f32[2048,512]{1,0:T(8,128)}) custom-call(f32[512,512]{1,0:T(8,128)S(1)} %polished.1.inverse_ref, f32[16,8,8,128]{3,2,1,0:T(8,128)S(1)} %broadcast_multiply_fusion.after_ref.mine_ref, f32[16,8,8,128]{3,2,1,0:T(8,128)S(1)} %collective-permute-done.8.other_ref, bf16[2048,512]{1,0:T(8,128)(2,1)} %get-tuple-element.21.z_hbm), custom_call_target="tpu_custom_call" | custom-call | flops 4600000000 | tf_op jit(solution)/shard_map/finished/pallas_call | solution.py:424
  (2 shorter events, 0.1 us)
Async XLA Ops:
  0.6 17.0 %collective-permute-start.3 = (f32[16,2048]{1,0:T(8,128)}, f32[16,2048]{1,0:T(8,128)S(1)}, u32[]{:S(2)}, u32[]{:S(2)}) collective-permute-start(f32[16,2048]{1,0:T(8,128)} %bitcast.9), channel_id=1, source_target_pairs={{0,6},{1,7},{2,0},{3,1},{4,2},{5,3},{6,4},{7,5},{8,14},{9,15},{10,... | collective-permute-start | bytes 393224 | tf_op jit(solution)/shard_map/ppermute | solution.py:455
  7.6 8.2 %collective-permute-start.2 = (f32[16,2048]{1,0:T(8,128)}, f32[16,2048]{1,0:T(8,128)S(1)}, u32[]{:S(2)}, u32[]{:S(2)}) collective-permute-start(f32[16,2048]{1,0:T(8,128)} %bitcast.10), channel_id=1, source_target_pairs={{0,2},{1,3},{2,4},{3,5},{4,6},{5,7},{6,0},{7,1},{8,10},{9,11},{10,... | collective-permute-start | bytes 393224 | tf_op jit(solution)/shard_map/ppermute | solution.py:455
  7.6 12.2 %collective-permute-start.1 = (f32[16,2048]{1,0:T(8,128)}, f32[16,2048]{1,0:T(8,128)S(1)}, u32[]{:S(2)}, u32[]{:S(2)}) collective-permute-start(f32[16,2048]{1,0:T(8,128)} %bitcast.11), channel_id=1, source_target_pairs={{0,7},{1,0},{2,1},{3,2},{4,3},{5,4},{6,5},{7,6},{8,15},{9,8},{10,9... | collective-permute-start | bytes 393224 | tf_op jit(solution)/shard_map/ppermute | solution.py:455
  10.7 9.1 %collective-permute-start = (f32[16,2048]{1,0:T(8,128)}, f32[16,2048]{1,0:T(8,128)S(1)}, u32[]{:S(2)}, u32[]{:S(2)}) collective-permute-start(f32[16,2048]{1,0:T(8,128)} %bitcast.12), channel_id=1, source_target_pairs={{0,1},{1,2},{2,3},{3,4},{4,5},{5,6},{6,7},{7,0},{8,9},{9,10},{10,1... | collective-permute-start | bytes 393224 | tf_op jit(solution)/shard_map/ppermute | solution.py:455
  15.8 13.8 %collective-permute-start.6 = (f32[16,2048]{1,0:T(8,128)S(1)}, f32[16,2048]{1,0:T(8,128)S(1)}, u32[]{:S(2)}, u32[]{:S(2)}) collective-permute-start(f32[16,2048]{1,0:T(8,128)S(1)} %collective-permute-done.2.refs_6_), channel_id=1, source_target_pairs={{0,2},{1,3},{2,4},{3,5},{4,6},{5,7},{6,0},{7,1},{8,10},{9,11},{10,... | collective-permute-start | bytes 393224 | tf_op jit(solution)/shard_map/ppermute | solution.py:455
  15.9 13.7 %collective-permute-start.4 = (f32[16,2048]{1,0:T(8,128)S(1)}, f32[16,2048]{1,0:T(8,128)S(1)}, u32[]{:S(2)}, u32[]{:S(2)}) collective-permute-start(f32[16,2048]{1,0:T(8,128)S(1)} %collective-permute-done.2.refs_6_), channel_id=1, source_target_pairs={{0,1},{1,2},{2,3},{3,4},{4,5},{5,6},{6,7},{7,0},{8,9},{9,10},{10,1... | collective-permute-start | bytes 393224 | tf_op jit(solution)/shard_map/ppermute | solution.py:455
  17.6 11.9 %collective-permute-start.5 = (f32[16,2048]{1,0:T(8,128)S(1)}, f32[16,2048]{1,0:T(8,128)S(1)}, u32[]{:S(2)}, u32[]{:S(2)}) collective-permute-start(f32[16,2048]{1,0:T(8,128)S(1)} %collective-permute-done.3.refs_7_), channel_id=1, source_target_pairs={{0,7},{1,0},{2,1},{3,2},{4,3},{5,4},{6,5},{7,6},{8,15},{9,8},{10,9... | collective-permute-start | bytes 393224 | tf_op jit(solution)/shard_map/ppermute | solution.py:455
  78.8 6.6 %collective-permute-start.7 = (f32[16,6,8,128]{3,2,1,0:T(8,128)S(1)}, f32[16,6,8,128]{3,2,1,0:T(8,128)S(1)}, u32[]{:S(2)}, u32[]{:S(2)}) collective-permute-start(f32[16,6,8,128]{3,2,1,0:T(8,128)S(1)} %all_to_all.22.refs_0_), channel_id=1, source_target_pairs={{0,8},{8,0},{1,9},{9,1},{2,10},{10,2},{3,11},{11,3},{4,12},{12,4},... | collective-permute-start | bytes 1179656 | tf_op jit(solution)/shard_map/ppermute | solution.py:476
  81.8 15.0 %all-to-all-start.2 = ((f32[16,8,8,128]{3,2,1,0:T(8,128)}), f32[16,8,8,128]{3,2,1,0:T(8,128)S(1)}, u32[]{:S(2)}, u32[]{:S(2)}) async-start(f32[16,8,8,128]{3,2,1,0:T(8,128)} %get-tuple-element.15), calls=%async_computation.2 | async-start | bytes 1048576 | tf_op jit(solution)/shard_map/all_to_all | solution.py:442
  96.8 6.6 %collective-permute-start.8 = (f32[16,8,8,128]{3,2,1,0:T(8,128)S(1)}, f32[16,8,8,128]{3,2,1,0:T(8,128)S(1)}, u32[]{:S(2)}, u32[]{:S(2)}) collective-permute-start(f32[16,8,8,128]{3,2,1,0:T(8,128)S(1)} %broadcast_multiply_fusion.after_ref.mine_ref), channel_id=1, source_target_pairs={{0,8},{8,0},{1,9},{9,1},{2,10},{10,2},{3,11},{11,3},{4,12},{12,4},... | collective-permute-start | bytes 1572872 | tf_op jit(solution)/shard_map/ppermute | solution.py:476

commit v5 on v4

--- a/solution.py
+++ b/solution.py
@@ -192,7 +192,7 @@
         out_ref[k] = total
 
 
-def inverse_kernel(scale, mine_ref, other_ref, gram_ref, inverse_ref, error_ref, scale_ref):
+def inverse_kernel(scale, mine_ref, other_ref, gram_ref, inverse_ref, scale_ref):
     scale_ref[...] = jnp.full(scale_ref.shape, scale, F32)
     across = M // TILE
     core = lax.axis_index("c")
@@ -229,8 +229,7 @@
     )
     factor = p[2] * eye + p[3] * gram + p[4] * square
     inverse_ref[...] = p[0] * eye + p[1] * gram + mirrored_product(split2(square), split2(factor))
-    error = improved(inverse_ref, g, 1.0 / last, 0.15)
-    error_ref[...] = jnp.broadcast_to(error, error_ref.shape)
+    improved(inverse_ref, g, 1.0 / last, 1e-2)
 
 
 def identity():
@@ -255,18 +254,15 @@
     return lax.while_loop(more, step, error)
 
 
-def polish_kernel(after_ref, gram_ref, start_ref, error_ref, inverse_ref):
-    gram = gram_ref[...]
-    inverse_ref[...] = start_ref[...]
-    improved(inverse_ref, split2(gram), error_ref[:1, :1], 1e-2)
-    x = inverse_ref[...]
-    rest = identity() - dot_pieces(split3(gram), split3(x))
+def polish_kernel(after_ref, gram_ref, start_ref, inverse_ref):
+    x = start_ref[...]
+    rest = identity() - dot_pieces(split3(gram_ref[...]), split3(x))
     low = rest.astype(BF16)
     rest = rest + dot(low, low)
     inverse_ref[...] = x + dot_pieces(split2(x), split2(rest))
 
 
-def finish_kernel(inverse_ref, mine_ref, other_ref, z_hbm, coef_ref, fitted_hbm, cross_ref, z, fitted, sems):
+def finish_kernel(inverse_ref, mine_ref, other_ref, z_hbm, coef_hbm, fitted_hbm, cross_ref, coef_ref, z, fitted, sems):
     n = z.shape[0]
     lines = z.shape[1]
     spans = [pl.ds(k * lines, lines) for k in range(n)]
@@ -283,8 +279,9 @@
             cross_ref[first : first + 8, TILE * j : TILE * (j + 1)] = tile
     coef = dot_pieces(x, split2(cross_ref[...]), 1)
     coef_ref[...] = coef
+    outs = [pltpu.make_async_copy(coef_ref, coef_hbm, sems.at[2 * n])]
+    outs[0].start()
     low = coef.astype(BF16)
-    outs = []
     for k, span in enumerate(spans):
         copies[k].wait()
         fitted[k] = dot(z[k], low)
@@ -396,24 +393,24 @@
     return pl.pallas_call(
         kernel,
         in_specs=[VMEM, VMEM],
-        out_specs=[VMEM] * 4,
-        out_shape=[shaped((M, M)), shaped((M, M)), shaped((8, TILE)), shaped((8, TILE))],
+        out_specs=[VMEM] * 3,
+        out_shape=[shaped((M, M))] * 2 + [shaped((8, TILE))],
         compiler_params=params(),
         cost_estimate=cost(9),
         name="inverted",
     )(mine, other)
 
 
-def polished(after, gram, start, error):
+def polished(after, gram, start):
     return pl.pallas_call(
         polish_kernel,
-        in_specs=[pl.BlockSpec(memory_space=pl.ANY)] + [VMEM] * 3,
+        in_specs=[pl.BlockSpec(memory_space=pl.ANY)] + [VMEM] * 2,
         out_specs=VMEM,
         out_shape=shaped((M, M)),
         compiler_params=params(),
         cost_estimate=cost(5),
         name="polished",
-    )(after, gram, start, error)
+    )(after, gram, start)
 
 
 def finished(inverse, mine, other, z):
@@ -424,13 +421,14 @@
     return pl.pallas_call(
         finish_kernel,
         in_specs=[VMEM, VMEM, VMEM, HBM],
-        out_specs=[VMEM, HBM],
+        out_specs=[HBM, HBM],
         out_shape=[shaped((M, M)), shaped((own, M))],
         scratch_shapes=[
             pltpu.VMEM((M, M), F32),
+            pltpu.VMEM((M, M), F32),
             pltpu.VMEM((n, lines, M), BF16),
             pltpu.VMEM((n, lines, M), F32),
-            pltpu.SemaphoreType.DMA((2 * n,)),
+            pltpu.SemaphoreType.DMA((2 * n + 1,)),
         ],
         compiler_params=params(),
         cost_estimate=cost(4),

time: 109 us -> 106 us (0.972)
  waiting for transfers between devices: 5.55 us -> 2.16 us
    pallas_call x1, Pallas kernels: 5.93 us -> 9.32 us  [inverted(): pl.pallas_call(kernel, in_specs=[VMEM, VMEM], out_specs=[VMEM] * 3, out_s...]
    all_to_all x1, waiting for transfers between devices: 5.42 us -> 2.04 us  [exchanged(): return lax.all_to_all(array, axes, 0, 0, tiled=True)]
    pallas_call x1, Pallas kernels: 5.4 us -> 3.07 us  [polished(): pl.pallas_call(polish_kernel, in_specs=[pl.BlockSpec(memory_space=pl.ANY)...]
  transfers between devices with their start and end apart: 10 -> 10, of which waited for: 2 -> 2; matrix products, arithmetic and copies ran while one was open for 0% -> 0% of each run, Pallas kernels for 24% -> 26%
where the time goes in v5:
time: 106 us
  blocking collectives  40.8 us (38%)
  Pallas kernels  39.8 us (38%)
  starting transfers between devices  22 us (21%)
  waiting for transfers between devices  2.16 us (2%)
    all_to_all x3, blocking collectives, exchanged(): return lax.all_to_all(array, axes, 0, 0, tiled=True)  40.8 us
    pallas_call x2, Pallas kernels, more_part(): pl.pallas_call(kernel, in_specs=[VMEM, VMEM, VMEM, HBM] + [VMEM] * n, out...  17.2 us
    ppermute x7, starting transfers between devices, moved(): return lax.ppermute(block, 'z', [(k, (k + by) % turn) for k in range(turn)])  14 us
    pallas_call x1, Pallas kernels, inverted(): pl.pallas_call(kernel, in_specs=[VMEM, VMEM], out_specs=[VMEM] * 3, out_s...  9.32 us
    pallas_call x1, Pallas kernels, own_part(): pl.pallas_call(kernel, in_specs=[HBM] * 5, out_specs=[VMEM, VMEM, VMEM, H...  5.09 us
    ppermute x2, starting transfers between devices, swapped(): return lax.ppermute(array, 'c', [(0, 1), (1, 0)])  4.42 us
    pallas_call x1, Pallas kernels, finished(): pl.pallas_call(finish_kernel, in_specs=[VMEM, VMEM, VMEM, HBM], out_specs...  4.2 us
    all_to_all x1, starting transfers between devices, exchanged(): return lax.all_to_all(array, axes, 0, 0, tiled=True)  3.57 us
  transfers between devices with their start and end apart: 10, of which 2 were waited for; matrix products, arithmetic and copies ran while one was open for 0% of the time, Pallas kernels for 26%

profile of v5, /device:TPU:1, one launch (start us, length us, event | category | flops | bytes accessed | tf_op | source)
XLA Modules:
  0.0 105.7 jit_solution(12865122936716567349)
XLA Ops:
  0.6 6.9 %collective-permute-start.3 = (f32[16,2048]{1,0:T(8,128)}, f32[16,2048]{1,0:T(8,128)S(1)}, u32[]{:S(2)}, u32[]{:S(2)}) collective-permute-start(f32[16,2048]{1,0:T(8,128)} %bitcast.9), channel_id=1, source_target_pairs={{0,6},{1,7},{2,0},{3,1},{4,2},{5,3},{6,4},{7,5},{8,14},{9,15},{10,... | collective-permute-start | bytes 393224 | tf_op jit(solution)/shard_map/ppermute | solution.py:453
  7.6 0.0 collective-permute-start.2
  7.6 3.1 %collective-permute-start.1 = (f32[16,2048]{1,0:T(8,128)}, f32[16,2048]{1,0:T(8,128)S(1)}, u32[]{:S(2)}, u32[]{:S(2)}) collective-permute-start(f32[16,2048]{1,0:T(8,128)} %bitcast.11), channel_id=1, source_target_pairs={{0,7},{1,0},{2,1},{3,2},{4,3},{5,4},{6,5},{7,6},{8,15},{9,8},{10,9... | collective-permute-start | bytes 393224 | tf_op jit(solution)/shard_map/ppermute | solution.py:453
  10.7 0.0 collective-permute-start
  10.7 5.1 %own_part.1 = (bf16[112,512]{1,0:T(8,128)(2,1)S(1)}, bf16[64,112]{1,0:T(8,128)(2,1)S(1)}, f32[128,512]{1,0:T(8,128)S(1)}, bf16[2048,512]{1,0:T(8,128)(2,1)}) custom-call(f32[16,4096]{1,0:T(8,128)} %bitcast.8, s32[1,512]{1,0:T(1,128)} %bitcast.14, f32[1,512]{1,0:T(1,128)} %bitcast.15, f32[16,2048]{1,0:T(8,128)} %bitcast.13, bf16[64,16384]{1,0:T(8,128)(2,1)} %bitcast.5), custom_call_target="tpu_custom_call" | custom-call | flops 5750000128 | tf_op jit(solution)/shard_map/own_part/pallas_call | solution.py:327
  15.8 0.0 collective-permute-done.2.refs_6_
  15.8 0.1 collective-permute-start.6
  15.9 1.7 %collective-permute-start.4 = (f32[16,2048]{1,0:T(8,128)S(1)}, f32[16,2048]{1,0:T(8,128)S(1)}, u32[]{:S(2)}, u32[]{:S(2)}) collective-permute-start(f32[16,2048]{1,0:T(8,128)S(1)} %collective-permute-done.2.refs_6_), channel_id=1, source_target_pairs={{0,1},{1,2},{2,3},{3,4},{4,5},{5,6},{6,7},{7,0},{8,9},{9,10},{10,1... | collective-permute-start | bytes 393224 | tf_op jit(solution)/shard_map/ppermute | solution.py:453
  17.6 0.0 collective-permute-done.3.refs_7_
  17.6 2.1 %collective-permute-start.5 = (f32[16,2048]{1,0:T(8,128)S(1)}, f32[16,2048]{1,0:T(8,128)S(1)}, u32[]{:S(2)}, u32[]{:S(2)}) collective-permute-start(f32[16,2048]{1,0:T(8,128)S(1)} %collective-permute-done.3.refs_7_), channel_id=1, source_target_pairs={{0,7},{1,0},{2,1},{3,2},{4,3},{5,4},{6,5},{7,6},{8,15},{9,8},{10,9... | collective-permute-start | bytes 393224 | tf_op jit(solution)/shard_map/ppermute | solution.py:453
  19.7 0.0 collective-permute-done.1.refs_5_
  19.7 0.1 collective-permute-done.refs_4_
  19.8 9.7 %more_part.2.refs_2_ = f32[128,512]{1,0:T(8,128)S(1)} custom-call(bf16[112,512]{1,0:T(8,128)(2,1)S(1)} %get-tuple-element.11.refs_0_, bf16[64,112]{1,0:T(8,128)(2,1)S(1)} %get-tuple-element.12.refs_1_, f32[128,512]{1,0:T(8,128)S(1)} %get-tuple-element.13.refs_2_, bf16[64,16384]{1,0:T(8,128)(2,1)} %bitcast.6, f32[16,2048]{1,0:T(8,128)S(1)} %collective-permute-done.refs_4_, ...), custom_call_target="tpu_custom_call" | custom-call | flops 11960000512 | tf_op jit(solution)/shard_map/more_part/pallas_call | solution.py:349
  29.5 0.0 collective-permute-done.5.refs_5_
  29.6 0.0 collective-permute-done.6.refs_6_
  29.6 0.0 collective-permute-done.4.refs_4_
  29.6 7.5 %more_part.3 = f32[32,16,128]{2,1,0:T(8,128)S(1)} custom-call(bf16[112,512]{1,0:T(8,128)(2,1)S(1)} %get-tuple-element.11.refs_0_, bf16[64,112]{1,0:T(8,128)(2,1)S(1)} %get-tuple-element.12.refs_1_, f32[128,512]{1,0:T(8,128)S(1)} %more_part.2.refs_2_, bf16[64,16384]{1,0:T(8,128)(2,1)} %bitcast.7, f32[16,2048]{1,0:T(8,128)S(1)} %collective-permute-done.4.refs_4_, ...), custom_call_target="tpu_custom_call" | custom-call | flops 8970000384 | tf_op jit(solution)/shard_map/more_part/pallas_call | solution.py:349
  37.1 18.7 %all_to_all.20.parts = f32[32,16,128]{2,1,0:T(8,128)S(1)} all-to-all(f32[32,16,128]{2,1,0:T(8,128)S(1)} %more_part.3), channel_id=1, replica_groups=mesh['y'=4,'x'=4,'c'=2,'z'=8] {'y','x','c'}, dimensions={0} | all-to-all | bytes 524288 | tf_op jit(solution)/shard_map/all_to_all | solution.py:440
  55.8 10.7 %all_to_all.21.parts_ref = f32[8,16,128]{2,1,0:T(8,128)S(1)} all-to-all(f32[8,16,128]{2,1,0:T(8,128)S(1)} %spread.1), channel_id=1, replica_groups=mesh['y'=4,'x'=4,'c'=2,'z'=8] {'z'}, dimensions={0} | all-to-all | bytes 131072 | tf_op jit(solution)/shard_map/all_to_all | solution.py:440
  66.6 0.8 packed.1
  67.4 11.3 %all_to_all.22.refs_0_ = f32[16,6,8,128]{3,2,1,0:T(8,128)S(1)} all-to-all(f32[16,6,8,128]{3,2,1,0:T(8,128)S(1)} %get-tuple-element.15), channel_id=1, replica_groups=mesh['y'=4,'x'=4,'c'=2,'z'=8] {'y','x'}, dimensions={0} | all-to-all | bytes 786432 | tf_op jit(solution)/shard_map/all_to_all | solution.py:440
  78.8 3.0 %collective-permute-start.7 = (f32[16,6,8,128]{3,2,1,0:T(8,128)S(1)}, f32[16,6,8,128]{3,2,1,0:T(8,128)S(1)}, u32[]{:S(2)}, u32[]{:S(2)}) collective-permute-start(f32[16,6,8,128]{3,2,1,0:T(8,128)S(1)} %all_to_all.22.refs_0_), channel_id=1, source_target_pairs={{0,8},{8,0},{1,9},{9,1},{2,10},{10,2},{3,11},{11,3},{4,12},{12,4},... | collective-permute-start | bytes 1179656 | tf_op jit(solution)/shard_map/ppermute | solution.py:474
  81.8 3.6 %all-to-all-start.2 = ((f32[16,8,8,128]{3,2,1,0:T(8,128)}), f32[16,8,8,128]{3,2,1,0:T(8,128)S(1)}, u32[]{:S(2)}, u32[]{:S(2)}) async-start(f32[16,8,8,128]{3,2,1,0:T(8,128)} %get-tuple-element.14), calls=%async_computation.2 | async-start | bytes 1048576 | tf_op jit(solution)/shard_map/all_to_all | solution.py:440
  85.3 0.0 collective-permute-done.7.refs_1_
  85.4 9.3 %inverted.1 = (f32[512,512]{1,0:T(8,128)S(1)}, f32[512,512]{1,0:T(8,128)S(1)}, f32[8,128]{1,0:T(8,128)S(1)}) custom-call(f32[16,6,8,128]{3,2,1,0:T(8,128)S(1)} %all_to_all.22.refs_0_, f32[16,6,8,128]{3,2,1,0:T(8,128)S(1)} %collective-permute-done.7.refs_1_), custom_call_target="tpu_custom_call" | custom-call | flops 10350000128 | tf_op jit(solution)/shard_map/inverted/pallas_call | solution.py:393
  94.7 2.0 %all-to-all-done.2 = f32[16,8,8,128]{3,2,1,0:T(8,128)S(1)} async-done(((f32[16,8,8,128]{3,2,1,0:T(8,128)}), f32[16,8,8,128]{3,2,1,0:T(8,128)S(1)}, u32[]{:S(2)}, u32[]{:S(2)}) %all-to-all-start.2) | async-done | bytes 524320 | tf_op jit(solution)/shard_map/all_to_all | solution.py:440
  96.8 1.4 %collective-permute-start.8 = (f32[16,8,8,128]{3,2,1,0:T(8,128)S(1)}, f32[16,8,8,128]{3,2,1,0:T(8,128)S(1)}, u32[]{:S(2)}, u32[]{:S(2)}) collective-permute-start(f32[16,8,8,128]{3,2,1,0:T(8,128)S(1)} %broadcast_multiply_fusion.after_ref.mine_ref), channel_id=1, source_target_pairs={{0,8},{8,0},{1,9},{9,1},{2,10},{10,2},{3,11},{11,3},{4,12},{12,4},... | collective-permute-start | bytes 1572872 | tf_op jit(solution)/shard_map/ppermute | solution.py:474
  98.2 3.1 %polished.1.inverse_ref = f32[512,512]{1,0:T(8,128)S(1)} custom-call(f32[16,8,8,128]{3,2,1,0:T(8,128)S(1)} %broadcast_multiply_fusion.after_ref.mine_ref, f32[512,512]{1,0:T(8,128)S(1)} %get-tuple-element.17.gram_ref, f32[512,512]{1,0:T(8,128)S(1)} %get-tuple-element.18.start_ref), custom_call_target="tpu_custom_call" | custom-call | flops 5750000128 | tf_op jit(solution)/shard_map/polished/pallas_call | solution.py:405
  101.3 0.0 collective-permute-done.8.other_ref
  101.3 4.2 %finished.1 = (f32[512,512]{1,0:T(8,128)}, f32[2048,512]{1,0:T(8,128)}) custom-call(f32[512,512]{1,0:T(8,128)S(1)} %polished.1.inverse_ref, f32[16,8,8,128]{3,2,1,0:T(8,128)S(1)} %broadcast_multiply_fusion.after_ref.mine_ref, f32[16,8,8,128]{3,2,1,0:T(8,128)S(1)} %collective-permute-done.8.other_ref, bf16[2048,512]{1,0:T(8,128)(2,1)} %get-tuple-element.19.z_hbm), custom_call_target="tpu_custom_call" | custom-call | flops 4600000000 | tf_op jit(solution)/shard_map/finished/pallas_call | solution.py:421
  (2 shorter events, 0.1 us)
Async XLA Ops:
  0.6 17.0 %collective-permute-start.3 = (f32[16,2048]{1,0:T(8,128)}, f32[16,2048]{1,0:T(8,128)S(1)}, u32[]{:S(2)}, u32[]{:S(2)}) collective-permute-start(f32[16,2048]{1,0:T(8,128)} %bitcast.9), channel_id=1, source_target_pairs={{0,6},{1,7},{2,0},{3,1},{4,2},{5,3},{6,4},{7,5},{8,14},{9,15},{10,... | collective-permute-start | bytes 393224 | tf_op jit(solution)/shard_map/ppermute | solution.py:453
  7.6 8.2 %collective-permute-start.2 = (f32[16,2048]{1,0:T(8,128)}, f32[16,2048]{1,0:T(8,128)S(1)}, u32[]{:S(2)}, u32[]{:S(2)}) collective-permute-start(f32[16,2048]{1,0:T(8,128)} %bitcast.10), channel_id=1, source_target_pairs={{0,2},{1,3},{2,4},{3,5},{4,6},{5,7},{6,0},{7,1},{8,10},{9,11},{10,... | collective-permute-start | bytes 393224 | tf_op jit(solution)/shard_map/ppermute | solution.py:453
  7.6 12.2 %collective-permute-start.1 = (f32[16,2048]{1,0:T(8,128)}, f32[16,2048]{1,0:T(8,128)S(1)}, u32[]{:S(2)}, u32[]{:S(2)}) collective-permute-start(f32[16,2048]{1,0:T(8,128)} %bitcast.11), channel_id=1, source_target_pairs={{0,7},{1,0},{2,1},{3,2},{4,3},{5,4},{6,5},{7,6},{8,15},{9,8},{10,9... | collective-permute-start | bytes 393224 | tf_op jit(solution)/shard_map/ppermute | solution.py:453
  10.7 9.1 %collective-permute-start = (f32[16,2048]{1,0:T(8,128)}, f32[16,2048]{1,0:T(8,128)S(1)}, u32[]{:S(2)}, u32[]{:S(2)}) collective-permute-start(f32[16,2048]{1,0:T(8,128)} %bitcast.12), channel_id=1, source_target_pairs={{0,1},{1,2},{2,3},{3,4},{4,5},{5,6},{6,7},{7,0},{8,9},{9,10},{10,1... | collective-permute-start | bytes 393224 | tf_op jit(solution)/shard_map/ppermute | solution.py:453
  15.8 13.8 %collective-permute-start.6 = (f32[16,2048]{1,0:T(8,128)S(1)}, f32[16,2048]{1,0:T(8,128)S(1)}, u32[]{:S(2)}, u32[]{:S(2)}) collective-permute-start(f32[16,2048]{1,0:T(8,128)S(1)} %collective-permute-done.2.refs_6_), channel_id=1, source_target_pairs={{0,2},{1,3},{2,4},{3,5},{4,6},{5,7},{6,0},{7,1},{8,10},{9,11},{10,... | collective-permute-start | bytes 393224 | tf_op jit(solution)/shard_map/ppermute | solution.py:453
  15.9 13.7 %collective-permute-start.4 = (f32[16,2048]{1,0:T(8,128)S(1)}, f32[16,2048]{1,0:T(8,128)S(1)}, u32[]{:S(2)}, u32[]{:S(2)}) collective-permute-start(f32[16,2048]{1,0:T(8,128)S(1)} %collective-permute-done.2.refs_6_), channel_id=1, source_target_pairs={{0,1},{1,2},{2,3},{3,4},{4,5},{5,6},{6,7},{7,0},{8,9},{9,10},{10,1... | collective-permute-start | bytes 393224 | tf_op jit(solution)/shard_map/ppermute | solution.py:453
  17.6 11.9 %collective-permute-start.5 = (f32[16,2048]{1,0:T(8,128)S(1)}, f32[16,2048]{1,0:T(8,128)S(1)}, u32[]{:S(2)}, u32[]{:S(2)}) collective-permute-start(f32[16,2048]{1,0:T(8,128)S(1)} %collective-permute-done.3.refs_7_), channel_id=1, source_target_pairs={{0,7},{1,0},{2,1},{3,2},{4,3},{5,4},{6,5},{7,6},{8,15},{9,8},{10,9... | collective-permute-start | bytes 393224 | tf_op jit(solution)/shard_map/ppermute | solution.py:453
  78.8 6.6 %collective-permute-start.7 = (f32[16,6,8,128]{3,2,1,0:T(8,128)S(1)}, f32[16,6,8,128]{3,2,1,0:T(8,128)S(1)}, u32[]{:S(2)}, u32[]{:S(2)}) collective-permute-start(f32[16,6,8,128]{3,2,1,0:T(8,128)S(1)} %all_to_all.22.refs_0_), channel_id=1, source_target_pairs={{0,8},{8,0},{1,9},{9,1},{2,10},{10,2},{3,11},{11,3},{4,12},{12,4},... | collective-permute-start | bytes 1179656 | tf_op jit(solution)/shard_map/ppermute | solution.py:474
  81.8 15.0 %all-to-all-start.2 = ((f32[16,8,8,128]{3,2,1,0:T(8,128)}), f32[16,8,8,128]{3,2,1,0:T(8,128)S(1)}, u32[]{:S(2)}, u32[]{:S(2)}) async-start(f32[16,8,8,128]{3,2,1,0:T(8,128)} %get-tuple-element.14), calls=%async_computation.2 | async-start | bytes 1048576 | tf_op jit(solution)/shard_map/all_to_all | solution.py:440
  96.8 4.5 %collective-permute-start.8 = (f32[16,8,8,128]{3,2,1,0:T(8,128)S(1)}, f32[16,8,8,128]{3,2,1,0:T(8,128)S(1)}, u32[]{:S(2)}, u32[]{:S(2)}) collective-permute-start(f32[16,8,8,128]{3,2,1,0:T(8,128)S(1)} %broadcast_multiply_fusion.after_ref.mine_ref), channel_id=1, source_target_pairs={{0,8},{8,0},{1,9},{9,1},{2,10},{10,2},{3,11},{11,3},{4,12},{12,4},... | collective-permute-start | bytes 1572872 | tf_op jit(solution)/shard_map/ppermute | solution.py:474
